TPU v7x, 512 devices: a whole 4x4x16 slice. The times are simulated.
512 devices in a mesh: req: 8 (over z_lo), section: 2 (over core), seq: 8 (over z_hi, y), tp: 4 (over x).
Axes of the slice: x: 4, y: 4, z: 16 (z_hi: 2, z_lo: 8; z = z_hi * 8 + z_lo), core: 2. Of those that a mesh axis runs over, the one named last changes fastest.
Arguments:
- hidden: bfloat16 [8192, 1536], P(('req', 'seq'), 'tp'), parts along dimension 0, may hold values from -2.5 to 2.5
- latent: float32 [8192, 64], P(('req', 'seq'), ('section', 'tp')), parts along dimension 0, may hold values from -6 to 6
- w_qkv: bfloat16 [2, 1536, 3, 1536], P('section', 'seq', None, 'tp'), may hold values from -0.15625 to 0.15625
- w_out: bfloat16 [2, 1536, 1536], P('section', 'tp'), may hold values from -0.625 to 0.625
- modulation: float32 [2, 3, 1536], P('section'), may hold values from -3 to 3
- final_mod: float32 [2, 1536], replicated, may hold values from -3 to 3
- w_final: bfloat16 [1536, 64], P(None, ('section', 'tp')), may hold values from -0.15625 to 0.15625
- stale_kv: bfloat16 [2, 2, 8192, 1536], P('section', None, ('req', 'seq'), 'tp'), parts along dimension 2, may hold values from -6 to 6
- text_kv: bfloat16 [2, 2, 1232, 1536], P('section', None, 'req', 'tp'), parts along dimension 2, as said below
- text_len: int32 [8], P('req'), parts along dimension 0, may hold values from 77 to 154
- patch_order: int32 [64, 4], P('req'), parts along dimension 0, may hold values from 0 to 3, each once within a row
- step_size: float32 [1], replicated, may hold values from -0.6 to -0.1
Outputs:
- latent_next: float32 [8192, 64], P(('req', 'seq'), ('section', 'tp')), parts along dimension 0
- new_kv: bfloat16 [2, 2, 8192, 1536], P('section', None, ('req', 'seq'), 'tp'), parts along dimension 2
There are 8 independent parts, one for each index of `req`. A program takes and returns all parts, laid end to end along the dimension named above; an argument that names none is the same for every part. Nothing has to cross between parts.
Inputs may be any that keep to these rules, and one draw needn't show every extreme that they name: Text tokens 0 to text_len - 1 are live, the rest of the 154 slots are padding. `patch_order`: each row is an ordering of the 4 patches of one index of seq. `text_kv`: keys and values of the text tokens.
All inputs are finite; a program needn't handle non-finite values.
Results may differ from a plain program's by a relative error of at most 0.015.
The roundings to bfloat16 on the way count: a program that leaves them out, or rounds other values in their place, can miss the bound.
Values may be sent and summed in bfloat16 or wider, within the bound.
A program may use at most 64 MiB of HBM per device.

v0:
```python
import jax
import jax.numpy as jnp
from jax import lax
from jax.sharding import PartitionSpec as P

HEAD = 64
MICRO = 4


def from_behind(value, axis, steps):
    count = lax.axis_size(axis)
    leading, last = (max(0, -steps), min(count, count - steps))
    return lax.ppermute(value, axis, [(source, source + steps) for source in range(leading, last)])


def layer_norm(row_block):
    row_block = row_block.astype(jnp.float32)
    center = row_block - jnp.mean(row_block, axis=-1, keepdims=True)
    spread = jnp.mean(center * center, axis=-1, keepdims=True)
    return center * lax.rsqrt(spread + 1e-06)


def modulate(row_block, shift_vec, scale_vec):
    return (layer_norm(row_block) * (1.0 + scale_vec) + shift_vec).astype(jnp.bfloat16)


def attend(queries, all_keys, all_values, text_keys, text_values, live_mask):
    factor = HEAD ** (-0.5)
    scores = (
        jnp.einsum("rhe,khe->hrk", queries, all_keys, preferred_element_type=jnp.float32) * factor
    )
    text_scores = (
        jnp.einsum("rhe,khe->hrk", queries, text_keys, preferred_element_type=jnp.float32) * factor
    )
    text_scores = jnp.where(live_mask[None, None, :], text_scores, -jnp.inf)
    peak_score = jnp.maximum(
        jnp.max(scores, axis=-1, keepdims=True), jnp.max(text_scores, axis=-1, keepdims=True)
    )
    weights = jnp.exp(scores - peak_score)
    text_weights = jnp.exp(text_scores - peak_score)
    total_mass = jnp.sum(weights, axis=-1, keepdims=True) + jnp.sum(
        text_weights, axis=-1, keepdims=True
    )
    prob_img = (weights / total_mass).astype(jnp.bfloat16)
    text_probs = (text_weights / total_mass).astype(jnp.bfloat16)
    attended = jnp.einsum("hrk,khe->rhe", prob_img, all_values, preferred_element_type=jnp.float32)
    attended = attended + jnp.einsum(
        "hrk,khe->rhe", text_probs, text_values, preferred_element_type=jnp.float32
    )
    return attended.astype(jnp.bfloat16).reshape(queries.shape[0], -1)


def take_fresh(new_kv_rows, column, is_valid, buffer, micro_ids):
    arrived = lax.all_gather(new_kv_rows[None], "seq", axis=0, tiled=True)
    hit_mask = (column[:, None] == micro_ids[None, :]) & is_valid
    return jnp.where(hit_mask[:, None, :, None, None], arrived[:, :, None], buffer)


def body(
    hidden,
    latent,
    w_qkv,
    w_out,
    modulation,
    final_mod,
    w_final,
    stale_kv,
    text_kv,
    text_len,
    patch_order,
    step_size,
):
    section_id = lax.axis_index("section")
    seq_id = lax.axis_index("seq")
    tp_id = lax.axis_index("tp")
    row_count, local_width = hidden.shape
    full_width = modulation.shape[2]
    patch_rows = row_count // MICRO
    seq_count = patch_order.shape[0]
    heads_here = local_width // HEAD
    shift_vec = modulation[0, 0]
    scale_vec = modulation[0, 1]
    gate_vec = modulation[0, 2]
    gate_here = lax.dynamic_slice_in_dim(gate_vec, tp_id * local_width, local_width)
    projection = lax.all_gather(w_qkv[0], "seq", axis=0, tiled=True).reshape(
        full_width, 3 * local_width
    )
    out_proj = w_out[0]
    text_keys = text_kv[0, 0].reshape(-1, heads_here, HEAD)
    text_values = text_kv[0, 1].reshape(-1, heads_here, HEAD)
    live_mask = jnp.arange(text_kv.shape[2], dtype=jnp.int32) < text_len[0]
    micro_ids = jnp.arange(MICRO, dtype=jnp.int32)
    seq_ids = jnp.arange(seq_count, dtype=jnp.int32)
    buffer = lax.all_gather(stale_kv, "seq", axis=0, tiled=True).reshape(
        seq_count, 2, MICRO, patch_rows, local_width
    )
    entry_blocks = hidden.reshape(MICRO, patch_rows, local_width)
    carried = jnp.zeros((patch_rows, local_width), jnp.bfloat16)
    finished = jnp.zeros((MICRO, patch_rows, local_width), jnp.bfloat16)
    for tick_index in range(MICRO + 1):
        micro_step = tick_index - section_id
        is_valid = (micro_step >= 0) & (micro_step < MICRO)
        clamped = jnp.clip(micro_step, 0, MICRO - 1)
        column = jnp.sum(jnp.where(micro_ids[None, :] == clamped, patch_order, 0), axis=1)
        my_patch = jnp.sum(jnp.where(seq_ids == seq_id, column, 0))
        picked = micro_ids == my_patch
        own_rows = lax.dynamic_index_in_dim(entry_blocks, my_patch, 0, keepdims=False)
        current = jnp.where(section_id == 0, own_rows, carried)
        full_rows = lax.all_gather(current, "tp", axis=1, tiled=True)
        normed = modulate(full_rows, shift_vec, scale_vec)
        joined = jnp.dot(normed, projection, preferred_element_type=jnp.float32).astype(
            jnp.bfloat16
        )
        queries = joined[:, :local_width].reshape(patch_rows, heads_here, HEAD)
        new_kv_rows = jnp.stack(
            [joined[:, local_width : 2 * local_width], joined[:, 2 * local_width :]]
        )
        buffer = take_fresh(new_kv_rows, column, is_valid, buffer, micro_ids)
        all_keys = buffer[:, 0].reshape(-1, heads_here, HEAD)
        all_values = buffer[:, 1].reshape(-1, heads_here, HEAD)
        attended = attend(queries, all_keys, all_values, text_keys, text_values, live_mask)
        partial_value = jnp.dot(attended, out_proj, preferred_element_type=jnp.float32)
        branch = lax.psum_scatter(partial_value, "tp", scatter_dimension=1, tiled=True)
        updated = (current.astype(jnp.float32) + gate_here * branch).astype(jnp.bfloat16)
        carried = from_behind(updated, "section", 1)
        finished = jnp.where((picked & is_valid)[:, None, None], updated[None], finished)
    returned = from_behind(finished, "section", -1)
    last_rows = jnp.where(section_id == 1, finished, returned).reshape(row_count, local_width)
    last_rows = lax.all_gather(last_rows, "tp", axis=1, tiled=True)
    final = modulate(last_rows, final_mod[0], final_mod[1])
    velocity = jnp.dot(final, w_final, preferred_element_type=jnp.float32)
    latent_next = latent + step_size[0] * velocity
    kv_next = lax.dynamic_index_in_dim(buffer, seq_id, 0, keepdims=False).reshape(
        1, 2, row_count, local_width
    )
    return (latent_next, kv_next)


def solution(mesh):
    return jax.shard_map(
        body,
        mesh=mesh,
        in_specs=(
            P(("req", "seq"), "tp"),
            P(("req", "seq"), ("section", "tp")),
            P("section", "seq", None, "tp"),
            P("section", "tp", None),
            P("section", None, None),
            P(),
            P(None, ("section", "tp")),
            P("section", None, ("req", "seq"), "tp"),
            P("section", None, "req", "tp"),
            P("req"),
            P("req", None),
            P(),
        ),
        out_specs=(P(("req", "seq"), ("section", "tp")), P("section", None, ("req", "seq"), "tp")),
        check_vma=False,
    )
```

profile of v0, /device:TPU:1, one launch (start us, length us, event | category | flops | bytes accessed | tf_op | source)
XLA Modules:
  0.0 890.5 jit_solution(9722535990750475162)
XLA Ops:
  11.9 1.5 fusion.215
  16.4 10.2 %all-gather = bf16[1,32,1536]{2,1,0:T(8,128)(2,1)S(1)} all-gather(bf16[1,32,384]{2,1,0:T(8,128)(2,1)S(1)} %dynamic-slice_select_fusion), channel_id=2, replica_groups=mesh['req'=8,'section'=2,'seq'=8,'tp'=4] {'tp'}, dimensions={2}, use_global_device_ids=true | all-gather | bytes 122880 | tf_op jit(solution)/shard_map/all_gather | solution.py:109
  28.2 147.5 %all-gather.12.cloned.1.call-done = bf16[1,1536,3,384]{3,1,2,0:T(8,128)(2,1)} async-done(((bf16[1,192,3,384]{3,1,2,0:T(8,128)(2,1)}), bf16[1,1536,3,384]{3,1,2,0:T(8,128)(2,1)}) %all-gather.12.cloned.1.call-update) | async-done | bytes 3538960 | tf_op jit(solution)/shard_map/all_gather | solution.py:85
  175.7 6.1 copy.101
  181.7 3.1 convolution_convert_fusion.4
  184.9 63.3 %all-gather.2 = bf16[16,32,384]{2,1,0:T(8,128)(2,1)S(1)} all-gather(bf16[2,32,384]{2,1,0:T(8,128)(2,1)S(1)} %pad_maximum_fusion), channel_id=4, replica_groups=mesh['req'=8,'section'=2,'seq'=8,'tp'=4] {'seq'}, dimensions={0}, use_global_device_ids=true | all-gather | bytes 442368 | tf_op jit(solution)/shard_map/all_gather | solution.py:54
  248.2 30.0 %all-gather.10.cloned.1.call-done = bf16[8,2,128,384]{3,2,1,0:T(8,128)(2,1)} async-done(((bf16[1,2,128,384]{3,2,1,0:T(8,128)(2,1)}), bf16[8,2,128,384]{3,2,1,0:T(8,128)(2,1)}) %all-gather.10.cloned.1.call-update) | async-done | bytes 1572880 | tf_op jit(solution)/shard_map/all_gather | solution.py:94
  278.2 1.9 copy_select_fusion
  280.3 2.2 reshape_squeeze.37
  282.6 2.3 fusion.216
  287.7 2.1 reshape_squeeze.36
  291.4 2.3 fusion.92
  296.3 18.9 %reduce-scatter.6.cloned.1.call-done = f32[32,384]{1,0:T(8,128)} async-done(((f32[32,1536]{1,0:T(8,128)}), f32[32,384]{1,0:T(8,128)}) %reduce-scatter.6.cloned.1.call-update) | async-done | bytes 49168 | tf_op jit(solution)/shard_map/reduce_scatter | solution.py:123
  320.9 9.4 %all_gather.43 = bf16[32,1536]{1,0:T(8,128)(2,1)S(1)} all-gather(bf16[32,384]{1,0:T(8,128)(2,1)S(1)} %bitcast_select_fusion), channel_id=1, replica_groups=mesh['req'=8,'section'=2,'seq'=8,'tp'=4] {'tp'}, dimensions={1}, use_global_device_ids=true | all-gather | bytes 122880 | tf_op jit(solution)/shard_map/all_gather | solution.py:109
  330.7 3.2 convolution_convert_fusion.3
  334.6 58.9 %all-gather.3 = bf16[16,32,384]{2,1,0:T(8,128)(2,1)S(1)} all-gather(bf16[2,32,384]{2,1,0:T(8,128)(2,1)S(1)} %pad_maximum_fusion.1), channel_id=5, replica_groups=mesh['req'=8,'section'=2,'seq'=8,'tp'=4] {'seq'}, dimensions={0}, use_global_device_ids=true | all-gather | bytes 442368 | tf_op jit(solution)/shard_map/all_gather | solution.py:54
  395.6 3.7 reshape_squeeze.41
  399.4 1.5 reshape.370
  402.0 2.4 fusion.218
  406.5 3.7 reshape_squeeze.40
  410.2 2.4 fusion.89
  413.3 1.6 reshape.371
  414.8 1.7 fusion.41
  417.9 34.1 %reduce-scatter.8.cloned.1.call-done = f32[32,384]{1,0:T(8,128)} async-done(((f32[32,1536]{1,0:T(8,128)}), f32[32,384]{1,0:T(8,128)}) %reduce-scatter.8.cloned.1.call-update) | async-done | bytes 49168 | tf_op jit(solution)/shard_map/reduce_scatter | solution.py:123
  451.9 1.4 add_convert_fusion.3
  459.3 9.1 %all_gather.45 = bf16[32,1536]{1,0:T(8,128)(2,1)S(1)} all-gather(bf16[32,384]{1,0:T(8,128)(2,1)S(1)} %bitcast_select_fusion.1), channel_id=1, replica_groups=mesh['req'=8,'section'=2,'seq'=8,'tp'=4] {'tp'}, dimensions={1}, use_global_device_ids=true | all-gather | bytes 122880 | tf_op jit(solution)/shard_map/all_gather | solution.py:109
  468.8 3.1 convolution_convert_fusion.2
  472.6 58.6 %all-gather.4 = bf16[16,32,384]{2,1,0:T(8,128)(2,1)S(1)} all-gather(bf16[2,32,384]{2,1,0:T(8,128)(2,1)S(1)} %pad_maximum_fusion.2), channel_id=6, replica_groups=mesh['req'=8,'section'=2,'seq'=8,'tp'=4] {'seq'}, dimensions={0}, use_global_device_ids=true | all-gather | bytes 442368 | tf_op jit(solution)/shard_map/all_gather | solution.py:54
  531.2 1.4 broadcast_select_fusion.2
  533.9 3.7 reshape_squeeze.43
  537.6 1.5 reshape.372
  540.3 2.4 fusion.220
  544.7 3.7 reshape_squeeze.42
  548.4 2.4 fusion.86
  551.5 1.6 reshape.373
  553.1 1.7 fusion.39
  556.1 35.6 %reduce-scatter.10.cloned.1.call-done = f32[32,384]{1,0:T(8,128)} async-done(((f32[32,1536]{1,0:T(8,128)}), f32[32,384]{1,0:T(8,128)}) %reduce-scatter.10.cloned.1.call-update) | async-done | bytes 49168 | tf_op jit(solution)/shard_map/reduce_scatter | solution.py:123
  591.7 1.4 add_convert_fusion.2
  599.1 9.3 %all_gather.47 = bf16[32,1536]{1,0:T(8,128)(2,1)S(1)} all-gather(bf16[32,384]{1,0:T(8,128)(2,1)S(1)} %bitcast_select_fusion.2), channel_id=1, replica_groups=mesh['req'=8,'section'=2,'seq'=8,'tp'=4] {'tp'}, dimensions={1}, use_global_device_ids=true | all-gather | bytes 122880 | tf_op jit(solution)/shard_map/all_gather | solution.py:109
  608.8 3.2 convolution_convert_fusion.1
  612.6 58.8 %all-gather.5 = bf16[16,32,384]{2,1,0:T(8,128)(2,1)S(1)} all-gather(bf16[2,32,384]{2,1,0:T(8,128)(2,1)S(1)} %pad_maximum_fusion.3), channel_id=7, replica_groups=mesh['req'=8,'section'=2,'seq'=8,'tp'=4] {'seq'}, dimensions={0}, use_global_device_ids=true | all-gather | bytes 442368 | tf_op jit(solution)/shard_map/all_gather | solution.py:54
  671.4 1.8 broadcast_select_fusion.1
  673.2 1.4 fusion.211
  674.6 3.7 reshape_squeeze.45
  678.3 1.5 reshape.374
  681.0 2.4 fusion.222
  685.4 3.7 reshape_squeeze.44
  689.2 2.4 fusion.83
  692.2 1.5 reshape.375
  693.8 1.7 fusion.37
  699.4 32.5 %reduce-scatter.12.cloned.1.call-done = f32[32,384]{1,0:T(8,128)} async-done(((f32[32,1536]{1,0:T(8,128)}), f32[32,384]{1,0:T(8,128)}) %reduce-scatter.12.cloned.1.call-update) | async-done | bytes 49168 | tf_op jit(solution)/shard_map/reduce_scatter | solution.py:123
  731.9 1.4 add_convert_fusion.1
  739.3 9.1 %all_gather.49 = bf16[32,1536]{1,0:T(8,128)(2,1)S(1)} all-gather(bf16[32,384]{1,0:T(8,128)(2,1)S(1)} %bitcast_select_fusion.3), channel_id=1, replica_groups=mesh['req'=8,'section'=2,'seq'=8,'tp'=4] {'tp'}, dimensions={1}, use_global_device_ids=true | all-gather | bytes 122880 | tf_op jit(solution)/shard_map/all_gather | solution.py:109
  748.8 3.2 convolution_convert_fusion
  752.6 59.5 %all-gather.6 = bf16[16,32,384]{2,1,0:T(8,128)(2,1)S(1)} all-gather(bf16[2,32,384]{2,1,0:T(8,128)(2,1)S(1)} %pad_maximum_fusion.4), channel_id=8, replica_groups=mesh['req'=8,'section'=2,'seq'=8,'tp'=4] {'seq'}, dimensions={0}, use_global_device_ids=true | all-gather | bytes 442368 | tf_op jit(solution)/shard_map/all_gather | solution.py:54
  812.1 1.9 broadcast_select_fusion
  815.2 2.2 reshape_squeeze.47
  817.8 2.3 fusion.224
  820.8 2.2 reshape_squeeze.46
  823.1 2.2 fusion.80
  829.1 33.1 %reduce-scatter.14.cloned.1.call-done = f32[32,384]{1,0:T(8,128)} async-done(((f32[32,1536]{1,0:T(8,128)}), f32[32,384]{1,0:T(8,128)}) %reduce-scatter.14.cloned.1.call-update) | async-done | bytes 49168 | tf_op jit(solution)/shard_map/reduce_scatter | solution.py:123
  863.9 4.8 collective-permute-start.4
  868.7 1.6 constant_dynamic-slice_fusion
  871.3 11.0 %all_gather.51 = bf16[128,1536]{1,0:T(8,128)(2,1)S(1)} all-gather(bf16[128,384]{1,0:T(8,128)(2,1)S(1)} %bitcast.206), channel_id=1, replica_groups=mesh['req'=8,'section'=2,'seq'=8,'tp'=4] {'tp'}, dimensions={1}, use_global_device_ids=true | all-gather | bytes 491520 | tf_op jit(solution)/shard_map/all_gather | solution.py:129
  (258 shorter events, 64.4 us)
Async XLA Ops:
  7.2 286.7 %copy-start = (bf16[1,384,1536]{2,1,0:T(8,128)(2,1)S(1)}, bf16[1,384,1536]{2,1,0:T(8,128)(2,1)}, u32[]{:S(2)}) copy-start(bf16[1,384,1536]{2,1,0:T(8,128)(2,1)} %param.15) | copy-start | bytes 3538948
  7.2 20.4 %copy-start.43 = (f32[1,3,1536]{2,0,1:T(1,128)S(1)}, f32[1,3,1536]{2,0,1:T(1,128)}, u32[]{:S(2)}) copy-start(f32[1,3,1536]{2,0,1:T(1,128)} %param.16) | copy-start | bytes 55300
  7.2 168.5 %all-gather.12.cloned.1.call-start = ((), (), s32[]{:S(2)}) async-start(), calls=%async_computation.11 | async-start | bytes 3981312 | tf_op jit(solution)/shard_map/all_gather | solution.py:85
  7.9 270.3 %all-gather.10.cloned.1.call-start = ((), (), s32[]{:S(2)}) async-start(), calls=%async_computation.5 | async-start | bytes 1769472 | tf_op jit(solution)/shard_map/all_gather | solution.py:94
  8.7 306.5 %reduce-scatter.6.cloned.1.call-start = ((), (), s32[]{:S(2)}) async-start(), calls=%async_computation.6 | async-start | bytes 245760 | tf_op jit(solution)/shard_map/reduce_scatter | solution.py:123
  13.5 271.4 %copy-start.3 = (bf16[1,1,154,384]{2,3,1,0:T(8,128)(2,1)}, bf16[1,1,154,384]{2,3,1,0:T(8,128)(2,1)S(1)}, u32[]{:S(2)}) copy-start(bf16[1,1,154,384]{2,3,1,0:T(8,128)(2,1)S(1)} %copy.106) | copy-start | bytes 354820
  27.6 250.6 %copy-start.34 = (pred[8,4]{1,0:T(8,128)(4,1)}, pred[8,4]{1,0:T(8,128)(4,1)S(1)}, u32[]{:S(2)}) copy-start(pred[8,4]{1,0:T(8,128)(4,1)S(1)} %fusion.204) | copy-start | bytes 100
  282.6 2.3 copy-start.13
  287.7 2.8 copy-start.22
  293.7 1.9 copy-start.57
  293.7 21.5 %copy-start.16 = (bf16[128,384]{1,0:T(8,128)(2,1)S(1)}, bf16[128,384]{1,0:T(8,128)(2,1)}, u32[]{:S(2)}) copy-start(bf16[128,384]{1,0:T(8,128)(2,1)} %param.12) | copy-start | bytes 294916
  294.9 157.0 %reduce-scatter.8.cloned.1.call-start = ((), (), s32[]{:S(2)}) async-start(), calls=%async_computation.7 | async-start | bytes 245760 | tf_op jit(solution)/shard_map/reduce_scatter | solution.py:123
  295.7 24.2 %copy-start.28 = (f32[384]{0:T(512)}, f32[384]{0:T(512)S(1)}, u32[]{:S(2)}) copy-start(f32[384]{0:T(512)S(1)} %fusion.209) | copy-start | bytes 4612
  316.0 14.6 %copy-start.14 = (bf16[32,384]{1,0:T(8,128)(2,1)}, bf16[32,384]{1,0:T(8,128)(2,1)S(1)}, u32[]{:S(2)}) copy-start(bf16[32,384]{1,0:T(8,128)(2,1)S(1)} %fusion.193) | copy-start | bytes 73732
  316.0 4.9 collective-permute-start
  320.9 9.8 %copy-start.19 = (bf16[32,384]{1,0:T(8,128)(2,1)}, bf16[32,384]{1,0:T(8,128)(2,1)S(1)}, u32[]{:S(2)}) copy-start(bf16[32,384]{1,0:T(8,128)(2,1)S(1)} %bitcast_select_fusion) | copy-start | bytes 73732
  330.7 62.8 %copy-start.1 = (bf16[8,2,128,384]{3,2,1,0:T(8,128)(2,1)S(1)}, bf16[8,2,128,384]{3,2,1,0:T(8,128)(2,1)}, u32[]{:S(2)}) copy-start(bf16[8,2,128,384]{3,2,1,0:T(8,128)(2,1)} %all-gather.10.cloned.1.call-done) | copy-start | bytes 4718596
  330.7 62.8 %copy-start.35 = (pred[8,4]{1,0:T(8,128)(4,1)S(1)}, pred[8,4]{1,0:T(8,128)(4,1)}, u32[]{:S(2)}) copy-start(pred[8,4]{1,0:T(8,128)(4,1)} %copy-done.34) | copy-start | bytes 100
  330.7 62.8 %copy-start.39 = (pred[8,4]{1,0:T(8,128)(4,1)S(1)}, pred[8,4]{1,0:T(8,128)(4,1)}, u32[]{:S(2)}) copy-start(pred[8,4]{1,0:T(8,128)(4,1)} %fusion.205) | copy-start | bytes 100
  402.0 3.6 copy-start.23
  404.4 2.1 copy-start.31
  416.6 175.1 %reduce-scatter.10.cloned.1.call-start = ((), (), s32[]{:S(2)}) async-start(), calls=%async_computation.8 | async-start | bytes 245760 | tf_op jit(solution)/shard_map/reduce_scatter | solution.py:123
  453.4 5.2 collective-permute-start.1
  459.3 9.4 %copy-start.20 = (bf16[32,384]{1,0:T(8,128)(2,1)}, bf16[32,384]{1,0:T(8,128)(2,1)S(1)}, u32[]{:S(2)}) copy-start(bf16[32,384]{1,0:T(8,128)(2,1)S(1)} %bitcast_select_fusion.1) | copy-start | bytes 73732
  468.8 62.4 %copy-start.36 = (pred[8,4]{1,0:T(8,128)(4,1)S(1)}, pred[8,4]{1,0:T(8,128)(4,1)}, u32[]{:S(2)}) copy-start(pred[8,4]{1,0:T(8,128)(4,1)} %copy-done.34) | copy-start | bytes 100
  468.8 62.4 %copy-start.40 = (pred[8,4]{1,0:T(8,128)(4,1)S(1)}, pred[8,4]{1,0:T(8,128)(4,1)}, u32[]{:S(2)}) copy-start(pred[8,4]{1,0:T(8,128)(4,1)} %fusion.205) | copy-start | bytes 100
  468.8 62.4 %copy-start.44 = (pred[8,4]{1,0:T(8,128)(4,1)S(1)}, pred[8,4]{1,0:T(8,128)(4,1)}, u32[]{:S(2)}) copy-start(pred[8,4]{1,0:T(8,128)(4,1)} %fusion.206) | copy-start | bytes 100
  531.2 1.4 copy-start.5
  540.2 3.6 copy-start.24
  542.7 2.1 copy-start.32
  554.8 177.1 %reduce-scatter.12.cloned.1.call-start = ((), (), s32[]{:S(2)}) async-start(), calls=%async_computation.9 | async-start | bytes 245760 | tf_op jit(solution)/shard_map/reduce_scatter | solution.py:123
  593.1 5.2 collective-permute-start.2
  599.1 9.6 %copy-start.21 = (bf16[32,384]{1,0:T(8,128)(2,1)}, bf16[32,384]{1,0:T(8,128)(2,1)S(1)}, u32[]{:S(2)}) copy-start(bf16[32,384]{1,0:T(8,128)(2,1)S(1)} %bitcast_select_fusion.2) | copy-start | bytes 73732
  608.7 62.7 %copy-start.6 = (bf16[16,32,384]{2,1,0:T(8,128)(2,1)S(1)}, bf16[16,32,384]{2,1,0:T(8,128)(2,1)}, u32[]{:S(2)}) copy-start(bf16[16,32,384]{2,1,0:T(8,128)(2,1)} %copy-done.5) | copy-start | bytes 1179652
  608.7 62.7 %copy-start.37 = (pred[8,4]{1,0:T(8,128)(4,1)S(1)}, pred[8,4]{1,0:T(8,128)(4,1)}, u32[]{:S(2)}) copy-start(pred[8,4]{1,0:T(8,128)(4,1)} %copy-done.34) | copy-start | bytes 100
  608.7 62.7 %copy-start.41 = (pred[8,4]{1,0:T(8,128)(4,1)S(1)}, pred[8,4]{1,0:T(8,128)(4,1)}, u32[]{:S(2)}) copy-start(pred[8,4]{1,0:T(8,128)(4,1)} %fusion.205) | copy-start | bytes 100
  608.7 62.7 %copy-start.45 = (pred[8,4]{1,0:T(8,128)(4,1)S(1)}, pred[8,4]{1,0:T(8,128)(4,1)}, u32[]{:S(2)}) copy-start(pred[8,4]{1,0:T(8,128)(4,1)} %fusion.206) | copy-start | bytes 100
  608.8 62.7 %copy-start.49 = (pred[8,4]{1,0:T(8,128)(4,1)S(1)}, pred[8,4]{1,0:T(8,128)(4,1)}, u32[]{:S(2)}) copy-start(pred[8,4]{1,0:T(8,128)(4,1)} %fusion.207) | copy-start | bytes 100
  671.4 1.8 copy-start.8
  681.0 3.6 copy-start.25
  683.4 2.1 copy-start.33
  695.6 166.7 %reduce-scatter.14.cloned.1.call-start = ((), (), s32[]{:S(2)}) async-start(), calls=%async_computation.10 | async-start | bytes 245760 | tf_op jit(solution)/shard_map/reduce_scatter | solution.py:123
  733.3 5.2 collective-permute-start.3
  739.3 9.4 %copy-start.17 = (bf16[32,384]{1,0:T(8,128)(2,1)}, bf16[32,384]{1,0:T(8,128)(2,1)S(1)}, u32[]{:S(2)}) copy-start(bf16[32,384]{1,0:T(8,128)(2,1)S(1)} %bitcast_select_fusion.3) | copy-start | bytes 73732
  748.7 63.4 %copy-start.7 = (bf16[16,32,384]{2,1,0:T(8,128)(2,1)S(1)}, bf16[16,32,384]{2,1,0:T(8,128)(2,1)}, u32[]{:S(2)}) copy-start(bf16[16,32,384]{2,1,0:T(8,128)(2,1)} %copy-done.5) | copy-start | bytes 1179652
  748.7 63.4 %copy-start.9 = (bf16[16,32,384]{2,1,0:T(8,128)(2,1)S(1)}, bf16[16,32,384]{2,1,0:T(8,128)(2,1)}, u32[]{:S(2)}) copy-start(bf16[16,32,384]{2,1,0:T(8,128)(2,1)} %copy-done.8) | copy-start | bytes 1179652
  748.7 63.4 %copy-start.38 = (pred[8,4]{1,0:T(8,128)(4,1)S(1)}, pred[8,4]{1,0:T(8,128)(4,1)}, u32[]{:S(2)}) copy-start(pred[8,4]{1,0:T(8,128)(4,1)} %copy-done.34) | copy-start | bytes 100
  748.7 63.4 %copy-start.42 = (pred[8,4]{1,0:T(8,128)(4,1)S(1)}, pred[8,4]{1,0:T(8,128)(4,1)}, u32[]{:S(2)}) copy-start(pred[8,4]{1,0:T(8,128)(4,1)} %fusion.205) | copy-start | bytes 100
  748.7 63.4 %copy-start.46 = (pred[8,4]{1,0:T(8,128)(4,1)S(1)}, pred[8,4]{1,0:T(8,128)(4,1)}, u32[]{:S(2)}) copy-start(pred[8,4]{1,0:T(8,128)(4,1)} %fusion.206) | copy-start | bytes 100
  748.8 63.4 %copy-start.50 = (pred[8,4]{1,0:T(8,128)(4,1)S(1)}, pred[8,4]{1,0:T(8,128)(4,1)}, u32[]{:S(2)}) copy-start(pred[8,4]{1,0:T(8,128)(4,1)} %fusion.207) | copy-start | bytes 100
  748.8 63.4 %copy-start.51 = (pred[8,4]{1,0:T(8,128)(4,1)S(1)}, pred[8,4]{1,0:T(8,128)(4,1)}, u32[]{:S(2)}) copy-start(pred[8,4]{1,0:T(8,128)(4,1)} %fusion.208) | copy-start | bytes 100
  815.2 2.2 copy-start.27
  815.2 2.3 copy-start.4
  815.2 2.3 copy-start.47
  817.8 2.8 copy-start.26
  825.3 3.8 copy-start.48
  825.3 36.9 %copy-start.18 = (bf16[32,384]{1,0:T(8,128)(2,1)S(1)}, bf16[32,384]{1,0:T(8,128)(2,1)}, u32[]{:S(2)}) copy-start(bf16[32,384]{1,0:T(8,128)(2,1)} %copy-done.17) | copy-start | bytes 73732
  825.3 36.9 %copy-start.29 = (f32[384]{0:T(512)S(1)}, f32[384]{0:T(512)}, u32[]{:S(2)}) copy-start(f32[384]{0:T(512)} %copy-done.28) | copy-start | bytes 4612
  825.3 37.7 %copy-start.15 = (bf16[32,384]{1,0:T(8,128)(2,1)S(1)}, bf16[32,384]{1,0:T(8,128)(2,1)}, u32[]{:S(2)}) copy-start(bf16[32,384]{1,0:T(8,128)(2,1)} %copy-done.14) | copy-start | bytes 73732
  825.3 37.7 %copy-start.55 = (pred[4]{0:T(512)(128)(4,1)S(1)}, pred[4]{0:T(512)(128)(4,1)}, u32[]{:S(2)}) copy-start(pred[4]{0:T(512)(128)(4,1)} %compare_and_fusion.3) | copy-start | bytes 16
  825.4 37.7 %copy-start.56 = (pred[4]{0:T(512)(128)(4,1)S(1)}, pred[4]{0:T(512)(128)(4,1)}, u32[]{:S(2)}) copy-start(pred[4]{0:T(512)(128)(4,1)} %compare_and_fusion.4) | copy-start | bytes 16
  826.5 56.2 %copy-start.58 = (bf16[1536,8]{0,1:T(8,128)(2,1)S(1)}, bf16[1536,8]{0,1:T(8,128)(2,1)}, u32[]{:S(2)}) copy-start(bf16[1536,8]{0,1:T(8,128)(2,1)} %param.18) | copy-start | bytes 73732
  826.5 56.2 %copy-start.59 = (f32[128,8]{0,1:T(8,128)S(1)}, f32[128,8]{0,1:T(8,128)}, u32[]{:S(2)}) copy-start(f32[128,8]{0,1:T(8,128)} %param.13) | copy-start | bytes 12292
  863.9 6.4 collective-permute-start.4
  (8 other events, 7.3 us)
Sparse Core Ops, SparseCore 0:
  11.2 164.4 all-gather.11
  178.8 99.2 all-gather.9
  295.0 20.1 reduce-scatter.5
  416.7 35.1 reduce-scatter.7
  555.0 36.6 reduce-scatter.9
  695.7 36.1 reduce-scatter.11
  826.7 35.5 reduce-scatter.13
where the time goes:
time: 894 us; the launch traced here: 890 us
  blocking collectives  357 us (40%)
  waiting for transfers between devices  336 us (38%)
  local copies, waits for them, and re-layouts  63.6 us (7%)
  matrix products  56.2 us (6%)
  other arithmetic  41.2 us (5%)
  between operations  26 us (3%)
  starting transfers between devices  10.2 us (1%)
    all_gather x5, blocking collectives, take_fresh(): arrived = lax.all_gather(new_kv_rows[None], 'seq', axis=0, tiled=True)  299 us
    reduce_scatter x5, waiting for transfers between devices, body(): lax.psum_scatter(partial_value, 'tp', scatter_dimension=1, tiled=True)  154 us
    all_gather x1, waiting for transfers between devices, body(): lax.all_gather(w_qkv[0], 'seq', axis=0, tiled=True)  147 us
    all_gather x5, blocking collectives, body(): full_rows = lax.all_gather(current, 'tp', axis=1, tiled=True)  47.1 us
    all_gather x1, waiting for transfers between devices, body(): lax.all_gather(stale_kv, 'seq', axis=0, tiled=True)  30 us
  transfers between devices with their start and end apart: 12, of which 11 were waited for; matrix products, arithmetic and copies ran while one was open for 4% of the time, Pallas kernels for 0%

commit v1 on v0

v1 whole, which is shorter than its diff:
```python
import jax
import jax.numpy as jnp
from jax import lax
from jax.experimental import pallas as pl
from jax.experimental.pallas import tpu as pltpu
from jax.sharding import PartitionSpec as P

HEAD = 64
MICRO = 4
NC = 4
MESH = pl.DeviceIdType.MESH
F32 = jnp.float32
BF16 = jnp.bfloat16


def dot(a, b):
    return jnp.dot(a, b, preferred_element_type=F32)


def dot_nt(a, b):
    return lax.dot_general(a, b, (((1,), (1,)), ((), ())), preferred_element_type=F32)


class Link:
    def __init__(self, send_sem, recv_sem):
        self.send_sem, self.recv_sem, self.used = send_sem, recv_sem, 0

    def take(self):
        index = self.used
        self.used += 1
        return index

    def make(self, index, src, dst, device):
        return pltpu.make_async_remote_copy(
            src_ref=src,
            dst_ref=dst,
            send_sem=self.send_sem.at[index],
            recv_sem=self.recv_sem.at[index],
            device_id=device,
            device_id_type=MESH,
        )


N_LINK = 64
N_LOCAL = 5


def kernel(
    order, tlen, step, hid_h, w_h, wo_h, st_h, tx_h, mod, fmod, wf, lat,
    out_lat, out_kv,
    hx, wv, kvf, kvs, tx, wo, nm, at, lhs, nkv, fin, acc, sbuf,
    send_sem, recv_sem, loc_sem, go_sem,
):
    sec = lax.axis_index("section")
    seq = lax.axis_index("seq")
    tp = lax.axis_index("tp")
    req = lax.axis_index("req")
    zh = seq // 4
    oh = 1 - zh
    y = seq % 4
    z = zh * 8 + req
    far = req // 4
    hop = 1 - 2 * far
    depth = req + far * (7 - 2 * req)
    xs = [(tp + k) % 4 for k in (1, 2, 3)]
    ys = [(y + k) % 4 for k in (1, 2, 3)]
    xfrom = [(tp + 4 - k) % 4 for k in (1, 2, 3)]
    yfrom = [(y + 4 - k) % 4 for k in (1, 2, 3)]
    xdev = [{"tp": v} for v in xs]
    ydev = [{"seq": zh * 4 + v} for v in ys]
    zdev = {"seq": (seq + 4) % 8}
    core = {"section": 1 - sec}
    znext = (z + hop + 16) % 16
    zprev = (z - hop + 16) % 16
    next_dev = {"seq": (znext // 8) * 4 + y, "req": znext % 8}
    prev_dev = {"seq": (zprev // 8) * 4 + y, "req": zprev % 8}

    barrier = pltpu.get_barrier_semaphore()
    for device in xdev + ydev + [zdev, core, next_dev, prev_dev]:
        pl.semaphore_signal(barrier, inc=1, device_id=device, device_id_type=MESH)
    pl.semaphore_wait(barrier, 10)

    link = Link(send_sem, recv_sem)
    half_rows = lambda h: pl.ds(h * 128, 128)
    i_hx = [link.take() for _ in range(3)]
    i_hz = link.take()
    i_hf = [link.take() for _ in range(3)]
    i_wy = [link.take() for _ in range(3)]
    i_ch = [link.take() for _ in range(NC)]
    i_ex = [link.take() for _ in range(NC)]
    i_wr = [[link.take() for _ in range(3)] for _ in range(NC)]
    i_sy = [link.take() for _ in range(3)]
    i_sz = link.take()
    i_sr = [link.take() for _ in range(3)]
    i_wo = [link.take() for _ in range(3)]
    i_kv = [link.take() for _ in range(3)]
    i_nk = link.take()
    i_ax = [link.take() for _ in range(3)]
    i_az = link.take()
    i_af = [link.take() for _ in range(3)]
    i_h1 = [link.take() for _ in range(4)]
    i_fn = link.take()

    def send(index, src, dst, device):
        link.make(index, src, dst, device).start()

    def arrived(index, dst):
        link.make(index, dst, dst, core).wait_recv()

    def sent(index, src):
        link.make(index, src, src, core).wait_send()

    def local(index, src, dst):
        return pltpu.make_async_copy(src, dst, loc_sem.at[index])

    hx_slot = lambda x, h: hx.at[x, half_rows(h), :]

    def hidden_send():
        send(i_hz, hid_h, hx_slot(tp, zh), zdev)
        for k in range(3):
            send(i_hx[k], hid_h, hx_slot(tp, zh), xdev[k])
        local(0, hid_h, hx_slot(tp, zh)).start()

    def hidden_own():
        local(0, hid_h, hx_slot(tp, zh)).wait()
        for k in range(3):
            arrived(i_hx[k], hx_slot(xfrom[k], zh))

    def hidden_forward():
        arrived(i_hz, hx_slot(tp, oh))
        for k in range(3):
            send(i_hf[k], hx_slot(tp, oh), hx_slot(tp, oh), xdev[k])

    def hidden_other():
        for k in range(3):
            arrived(i_hf[k], hx_slot(xfrom[k], oh))

    def hidden_sent():
        sent(i_hz, hid_h)
        for k in range(3):
            sent(i_hx[k], hid_h)
            sent(i_hf[k], hx_slot(tp, oh))

    CR = 192 // NC
    w_rows = lambda s: wv.at[pl.ds(s * 192, 192), :]
    w_piece = lambda s, c: wv.at[pl.ds(s * 192 + c * CR, CR), :]

    def weights_send():
        @pl.when(depth == 0)
        def _():
            for c in range(NC):
                pltpu.make_async_remote_copy(
                    src_ref=w_h.at[oh, pl.ds(c * CR, CR), :],
                    dst_ref=w_piece(seq, c),
                    send_sem=send_sem.at[i_ex[c]],
                    recv_sem=recv_sem.at[i_ch[c]],
                    device_id=prev_dev,
                    device_id_type=MESH,
                ).start()

        for k in range(3):
            send(i_wy[k], w_h.at[zh], w_rows(seq), ydev[k])
        local(1, w_h.at[zh], w_rows(seq)).start()

    oseq = oh * 4 + y

    def weights_relay():
        for c in range(NC):
            arrived(i_ch[c], w_piece(oseq, c))

            @pl.when(depth < 3)
            def _(c=c):
                send(i_ch[c], w_piece(oseq, c), w_piece(oseq, c), next_dev)

            for k in range(3):
                send(i_wr[c][k], w_piece(oseq, c), w_piece(oseq, c), ydev[k])

    def weights_near():
        local(1, w_h.at[zh], w_rows(seq)).wait()
        for k in range(3):
            arrived(i_wy[k], w_rows(zh * 4 + yfrom[k]))

    def weights_far():
        for c in range(NC):
            for k in range(3):
                arrived(i_wr[c][k], w_piece(oh * 4 + yfrom[k], c))

    def weights_sent():
        @pl.when(depth == 0)
        def _():
            for c in range(NC):
                sent(i_ex[c], w_h.at[oh, pl.ds(c * CR, CR), :])

        @pl.when(depth < 3)
        def _():
            for c in range(NC):
                sent(i_ch[c], w_piece(oseq, c))

        for k in range(3):
            sent(i_wy[k], w_rows(seq))
            for c in range(NC):
                sent(i_wr[c][k], w_piece(oseq, c))

    st_slot = lambda v, h: kvs.at[v, half_rows(h), :]

    def stale_z():
        send(i_sz, st_h.at[oh], st_slot(y, zh), zdev)

    def stale_y():
        for k in range(3):
            send(i_sy[k], st_h.at[zh], st_slot(y, zh), ydev[k])
        local(2, st_h.at[zh], st_slot(y, zh)).start()
        local(3, tx_h.at[zh], tx).start()

    def stale_relay():
        arrived(i_sz, st_slot(y, oh))
        for k in range(3):
            send(i_sr[k], st_slot(y, oh), st_slot(y, oh), ydev[k])

    def stale_all():
        local(2, st_h.at[zh], st_slot(y, zh)).wait()
        local(3, tx_h.at[zh], tx).wait()
        for k in range(3):
            arrived(i_sy[k], st_slot(yfrom[k], zh))
            arrived(i_sr[k], st_slot(yfrom[k], oh))

    def stale_sent():
        sent(i_sz, st_slot(y, zh))
        for k in range(3):
            sent(i_sy[k], st_slot(y, zh))
            sent(i_sr[k], st_slot(y, oh))

    wo_rows = lambda x: wo.at[pl.ds(x * 384, 384), :]

    def out_send():
        for k in range(3):
            send(i_wo[k], wo_h, wo_rows(tp), xdev[k])
        local(4, wo_h, wo_rows(tp)).start()

    def out_all():
        local(4, wo_h, wo_rows(tp)).wait()
        for k in range(3):
            arrived(i_wo[k], wo_rows(xfrom[k]))

    row_id = lax.broadcasted_iota(jnp.int32, (1, 256), 1)
    lane_seg = row_id // 32
    rank_of = [
        [sum(jnp.where(order[s, k] == p, k, 0) for k in range(1, MICRO)) for p in range(MICRO)]
        for s in range(8)
    ]
    col_seg = lax.broadcasted_iota(jnp.int32, (256, 1), 0) // 32
    qrank = jnp.zeros((256, 1), jnp.int32)
    kranks = []
    for v in range(4):
        krank = jnp.zeros((1, 256), jnp.int32)
        for j in range(8):
            scalar = rank_of[(j // 4) * 4 + v][j % 4]
            krank = jnp.where(lane_seg == j, scalar, krank)
            qrank = jnp.where((col_seg == j) & (y == v), scalar, qrank)
        kranks.append(krank)
    low = lax.broadcasted_iota(jnp.int32, (1, 128), 1) < HEAD
    text_live = lax.broadcasted_iota(jnp.int32, (1, 256), 1) < tlen[0]

    def norm_rows(r0, count, shift_ref, scale_ref, store):
        parts = [hx[c, pl.ds(r0, count), :].astype(F32) for c in range(4)]
        total = sum(jnp.sum(part, axis=-1, keepdims=True) for part in parts)
        mean = total * (1.0 / 1536)
        parts = [part - mean for part in parts]
        spread = sum(jnp.sum(part * part, axis=-1, keepdims=True) for part in parts)
        inv = lax.rsqrt(spread * (1.0 / 1536) + 1e-06)
        for c in range(4):
            lanes = slice(c * 384, (c + 1) * 384)
            value = parts[c] * inv * (1.0 + scale_ref(lanes)) + shift_ref(lanes)
            store(c, value.astype(BF16))

    def norm_block(h):
        for b in range(4):
            r0 = h * 128 + b * 32

            def store(c, value, r0=r0):
                nm[c // 2, pl.ds(r0, 32), (c % 2) * 384 : (c % 2) * 384 + 384] = value

            norm_rows(
                r0, 32, lambda l: mod[0:1, l], lambda l: mod[1:2, l], store
            )

    @pl.when(sec == 0)
    def _():
        hidden_send()
        weights_send()

        @pl.when(depth == 3)
        def _():
            hidden_forward()

        weights_relay()

        @pl.when(depth < 3)
        def _():
            hidden_forward()

        hidden_own()
        stale_z()
        stale_y()
        out_send()
        hidden_other()

    @pl.when(sec == 1)
    def _():
        pl.semaphore_wait(go_sem.at[0], 1)
        weights_send()
        stale_z()
        stale_y()
        pl.semaphore_wait(go_sem.at[1], 1)
        out_send()
        weights_relay()
        stale_relay()
        for n in range(4):
            arrived(i_h1[n], hx.at[n])

    norm_block(0)
    norm_block(1)
    weights_near()
    for c in range(5):
        lanes = slice(c * 128, c * 128 + 128)
        acc[:, lanes] = dot(nm[zh], wv[pl.ds(zh * 768, 768), lanes])
    weights_far()
    own = kvf.at[y]
    for c in range(5):
        lanes = slice(c * 128, c * 128 + 128)
        value = (acc[:, lanes] + dot(nm[oh], wv[pl.ds(oh * 768, 768), lanes])).astype(BF16)
        if c < 3:
            kvf[y, :, lanes] = value
        else:
            lhs[:, (c - 3) * 128 : (c - 2) * 128] = value
        if c == 2:
            for k in range(3):
                send(i_kv[k], own, own, ydev[k])
    send(i_nk, kvf.at[y, half_rows(oh), :], nkv, zdev)

    @pl.when(sec == 0)
    def _():
        pl.semaphore_signal(go_sem.at[0], inc=1, device_id=core, device_id_type=MESH)
        stale_relay()

    out_all()

    @pl.when(sec == 0)
    def _():
        pl.semaphore_signal(go_sem.at[1], inc=1, device_id=core, device_id_type=MESH)

    stale_all()
    for k in range(3):
        arrived(i_kv[k], kvf.at[yfrom[k]])

    heads = ((0, 0, 0), (0, 0, 1), (1, 1, 2))
    single_low = zh == 0

    def attend(rb):
        rows = slice(rb * 128, rb * 128 + 128)
        rank = qrank[rows]
        masks = [kranks[v] <= rank for v in range(4)]
        outs = []
        for j in range(3):
            tile = 0 if j < 2 else 1
            query = lhs[rows, tile * 128 : tile * 128 + 128].astype(F32) * (HEAD ** (-0.5))
            if j == 0:
                keep = low
            elif j == 1:
                keep = jnp.logical_not(low)
            else:
                keep = low == single_low
            query = jnp.where(keep, query, 0.0).astype(BF16)
            kl = slice(tile * 128, tile * 128 + 128)
            vl = slice(256, 384) if j < 2 else kl
            for v in range(4):
                fresh = dot_nt(query, kvf[v, :, kl])
                stale = dot_nt(query, kvs[v, :, kl])
                sbuf[:, v * 256 : v * 256 + 256] = jnp.where(masks[v], fresh, stale)
            text = dot_nt(query, tx[:, kl])
            sbuf[:, 1024:1280] = jnp.where(text_live, text, -1e30)
            scores = sbuf[...]
            peak = jnp.max(scores, axis=-1, keepdims=True)
            weights = jnp.exp(scores - peak)
            inv = 1.0 / jnp.sum(weights, axis=-1, keepdims=True)
            sbuf[...] = weights * inv
            total = dot(sbuf[:, 1024:1280].astype(BF16), tx[:, vl])
            for v in range(4):
                weights = sbuf[:, v * 256 : v * 256 + 256]
                fresh = jnp.where(masks[v], weights, 0.0).astype(BF16)
                stale = jnp.where(masks[v], 0.0, weights).astype(BF16)
                total = total + dot(fresh, kvf[v, :, vl]) + dot(stale, kvs[v, :, vl])
            outs.append(total)
        at[zh, tp, rows, :] = jnp.where(low, outs[0], outs[1]).astype(BF16)
        single = jnp.where(low == single_low, 0.0, outs[2])
        return single + pltpu.roll(single, HEAD, 1)

    first = attend(0)
    second = attend(1)
    at[zh, tp, 256:384, :] = jnp.where(low, first, second).astype(BF16)
    mine = at.at[zh, tp]
    send(i_az, mine, mine, zdev)
    for k in range(3):
        send(i_ax[k], mine, mine, xdev[k])

    arrived(i_nk, nkv)
    mine_kv = [kvf[y, half_rows(zh), c * 128 : c * 128 + 128].astype(F32) for c in range(3)]
    their_kv = [nkv[:, c * 128 : c * 128 + 128].astype(F32) for c in range(3)]
    first_kv = [jnp.where(zh == 0, a, b) for a, b in zip(mine_kv, their_kv)]
    second_kv = [jnp.where(zh == 0, b, a) for a, b in zip(mine_kv, their_kv)]
    out_kv[0, :, 0:128] = first_kv[0].astype(BF16)
    out_kv[0, :, 128:256] = jnp.where(low, first_kv[1], second_kv[1]).astype(BF16)
    out_kv[0, :, 256:384] = second_kv[0].astype(BF16)
    out_kv[1, :, 0:128] = first_kv[2].astype(BF16)
    out_kv[1, :, 128:256] = pltpu.roll(
        jnp.where(low, second_kv[1], first_kv[1]), HEAD, 1
    ).astype(BF16)
    out_kv[1, :, 256:384] = second_kv[2].astype(BF16)

    theirs = at.at[oh, tp]
    arrived(i_az, theirs)
    for k in range(3):
        send(i_af[k], theirs, theirs, xdev[k])
    for k in range(3):
        arrived(i_ax[k], at.at[zh, xfrom[k]])
    for k in range(3):
        arrived(i_af[k], at.at[oh, xfrom[k]])
    for x in range(4):
        lhs[:, x * 384 : x * 384 + 128] = at[0, x, 0:256, :]
        lhs[:, x * 384 + 256 : x * 384 + 384] = at[1, x, 0:256, :]
        a = at[0, x, 256:384, :].astype(F32)
        b = at[1, x, 256:384, :].astype(F32)
        tile = slice(x * 384 + 128, x * 384 + 256)
        lhs[0:128, tile] = jnp.where(low, a, pltpu.roll(b, HEAD, 1)).astype(BF16)
        lhs[128:256, tile] = jnp.where(low, pltpu.roll(a, HEAD, 1), b).astype(BF16)

    @pl.when(sec == 0)
    def _():
        hidden_sent()

    for n in range(4):
        lanes = slice(n * 384, n * 384 + 384)
        branch = dot(lhs[...], wo[:, lanes])
        hx[n] = (hx[n].astype(F32) + mod[2:3, lanes] * branch).astype(BF16)

        @pl.when(sec == 0)
        def _(n=n):
            send(i_h1[n], hx.at[n], hx.at[n], core)

    @pl.when(sec == 1)
    def _():
        for b in range(4):
            r0 = zh * 128 + b * 32

            def store(c, value, b=b):
                fin[b * 32 : b * 32 + 32, c * 384 : c * 384 + 384] = value

            norm_rows(r0, 32, lambda l: fmod[0:1, l], lambda l: fmod[1:2, l], store)
        send(i_fn, fin, fin, core)

    @pl.when(sec == 0)
    def _():
        arrived(i_fn, fin)

    out_lat[...] = lat[...] + step[0] * dot(fin[...], wf[...])

    @pl.when(sec == 0)
    def _():
        for n in range(4):
            sent(i_h1[n], hx.at[n])

    @pl.when(sec == 1)
    def _():
        sent(i_fn, fin)

    weights_sent()
    stale_sent()
    for k in range(3):
        sent(i_wo[k], wo_rows(tp))
        sent(i_kv[k], own)
        sent(i_ax[k], mine)
        sent(i_af[k], theirs)
    sent(i_nk, nkv)
    sent(i_az, mine)


def pair_of(block, half):
    return block[..., 0:128] if half == 0 else block[..., 256:384]


def kv_tiles(k, v, half):
    if half == 0:
        single = [k[..., 128:192], v[..., 128:192]]
    else:
        single = [v[..., 192:256], k[..., 192:256]]
    return [pair_of(k, half)] + single + [pair_of(v, half)]


def body(
    hidden, latent, w_qkv, w_out, modulation, final_mod, w_final, stale_kv, text_kv, text_len,
    patch_order, step_size,
):
    w = w_qkv[0]
    q, k, v = w[:, 0], w[:, 1], w[:, 2]
    weights = jnp.stack(
        [
            jnp.concatenate(kv_tiles(k, v, h) + [pair_of(q, h), q[:, 128:256]], axis=-1)
            for h in range(2)
        ]
    )
    stale = jnp.stack(
        [jnp.concatenate(kv_tiles(stale_kv[0, 0], stale_kv[0, 1], h), axis=-1) for h in range(2)]
    )
    text = jnp.stack(
        [jnp.concatenate(kv_tiles(text_kv[0, 0], text_kv[0, 1], h), axis=-1) for h in range(2)]
    )
    text = jnp.pad(text, ((0, 0), (0, 256 - text.shape[1]), (0, 0)))
    smem = pl.BlockSpec(memory_space=pltpu.SMEM)
    vmem = pl.BlockSpec(memory_space=pltpu.VMEM)
    any_ = pl.BlockSpec(memory_space=pl.ANY)
    lat_next, kv_next = pl.pallas_call(
        kernel,
        out_shape=(
            jax.ShapeDtypeStruct((128, 8), F32),
            jax.ShapeDtypeStruct((2, 128, 384), BF16),
        ),
        in_specs=[smem, smem, smem, any_, any_, any_, any_, any_, vmem, vmem, vmem, vmem],
        out_specs=(vmem, vmem),
        scratch_shapes=[
            pltpu.VMEM((4, 256, 384), BF16),
            pltpu.VMEM((1536, 640), BF16),
            pltpu.VMEM((4, 256, 384), BF16),
            pltpu.VMEM((4, 256, 384), BF16),
            pltpu.VMEM((256, 384), BF16),
            pltpu.VMEM((1536, 1536), BF16),
            pltpu.VMEM((2, 256, 768), BF16),
            pltpu.VMEM((2, 4, 384, 128), BF16),
            pltpu.VMEM((256, 1536), BF16),
            pltpu.VMEM((128, 384), BF16),
            pltpu.VMEM((128, 1536), BF16),
            pltpu.VMEM((256, 640), F32),
            pltpu.VMEM((128, 1280), F32),
            pltpu.SemaphoreType.DMA((N_LINK,)),
            pltpu.SemaphoreType.DMA((N_LINK,)),
            pltpu.SemaphoreType.DMA((N_LOCAL,)),
            pltpu.SemaphoreType.REGULAR((2,)),
        ],
        compiler_params=pltpu.CompilerParams(
            collective_id=0, has_side_effects=True, vmem_limit_bytes=48 << 20
        ),
        name="both_layers",
    )(
        patch_order, text_len, step_size, hidden, weights, w_out[0], stale, text, modulation[0],
        final_mod, w_final, latent,
    )
    return lat_next, kv_next[None]


def solution(mesh):
    return jax.shard_map(
        body,
        mesh=mesh,
        in_specs=(
            P(("req", "seq"), "tp"),
            P(("req", "seq"), ("section", "tp")),
            P("section", "seq", None, "tp"),
            P("section", "tp", None),
            P("section", None, None),
            P(),
            P(None, ("section", "tp")),
            P("section", None, ("req", "seq"), "tp"),
            P("section", None, "req", "tp"),
            P("req"),
            P("req", None),
            P(),
        ),
        out_specs=(P(("req", "seq"), ("section", "tp")), P("section", None, ("req", "seq"), "tp")),
        check_vma=False,
    )
```

time: 894 us -> 132 us (0.15)
  the two profiles are of different devices: /device:TPU:1 before, /device:TPU:113 now
where the time goes in v1:
time: 132 us
  Pallas kernels  124 us (94%)
  local copies, waits for them, and re-layouts  4.72 us (4%)
  between operations  2.22 us (2%)
    pallas_call x1, Pallas kernels, body(): pl.pallas_call(kernel, out_shape=(jax.ShapeDtypeStruct((128, 8), F32), ja...  124 us

profile of v1, /device:TPU:113, one launch (start us, length us, event | category | flops | bytes accessed | tf_op | source)
XLA Modules:
  0.0 131.8 jit_solution(12454340755180759458)
XLA Ops:
  0.6 1.1 slice_bitcast_fusion
  1.8 0.1 fusion.4
  1.9 0.1 slice.145
  2.0 0.0 copy-start.4
  2.0 0.1 concatenate.22
  2.1 0.1 maximum_bitcast_fusion
  2.2 0.0 copy-start.3
  2.2 0.1 pad_maximum_fusion.w_h
  2.3 0.6 copy-done.4
  2.9 0.1 fusion.9
  3.0 0.1 slice.154
  3.1 0.1 maximum_bitcast_fusion.3
  3.3 0.0 copy-done.3
  3.3 0.3 fusion.3
  3.6 0.0 copy-start.5
  3.7 0.0 copy-start.7
  3.7 0.0 copy-start.6
  3.7 0.0 copy-start.8
  3.7 0.0 copy-start
  3.7 0.0 copy-start.1
  3.7 0.0 copy-start.2
  3.7 0.1 fusion.7
  3.8 0.1 slice.161
  3.9 0.1 maximum_bitcast_fusion.2
  4.1 0.1 maximum_bitcast_fusion.1
  4.2 0.2 copy-done.5
  4.4 0.2 copy.17.wf
  4.6 0.0 copy-done.7
  4.6 0.1 copy.18.lat
  4.7 0.0 copy-done.6
  4.7 0.0 copy-done.8
  4.7 0.1 copy.16.order
  6.1 0.0 copy-done
  6.1 0.0 copy-done.1
  6.1 0.0 copy-done.2
  6.1 124.3 %both_layers.1 = (f32[128,8]{1,0:T(8,128)S(1)}, bf16[2,128,384]{2,1,0:T(8,128)(2,1)S(1)}) custom-call(s32[8,4]{1,0:T(8,128)S(1)} %copy.16.order, s32[1]{0:T(128)S(6)} %copy.28.tlen, f32[1]{0:T(128)S(6)} %copy.29.step, bf16[128,384]{1,0:T(8,128)(2,1)S(1)} %copy-done.1, bf16[2,192,640]{2,1,0:T(8,128)(2,1)S(1)} %pad_maximum_fusion.w_h, ...), custom_call_target="tpu_custom_call" | custom-call | tf_op jit(solution)/shard_map/both_layers/pallas_call | solution.py:521
  130.4 0.7 copy.19
  131.1 0.7 copy.30
  (15 shorter events, 0.2 us)
Async XLA Ops:
  2.0 0.9 copy-start.4
  2.2 1.0 copy-start.3
  3.6 0.7 copy-start.5
  3.7 0.9 copy-start.7
  3.7 1.0 copy-start.6
  3.7 1.0 copy-start.8
  3.7 2.4 %copy-start = (bf16[1,384,1536]{2,1,0:T(8,128)(2,1)S(1)}, bf16[1,384,1536]{2,1,0:T(8,128)(2,1)}, u32[]{:S(2)}) copy-start(bf16[1,384,1536]{2,1,0:T(8,128)(2,1)} %param.15) | copy-start | bytes 3538948
  3.7 2.4 %copy-start.1 = (bf16[128,384]{1,0:T(8,128)(2,1)S(1)}, bf16[128,384]{1,0:T(8,128)(2,1)}, u32[]{:S(2)}) copy-start(bf16[128,384]{1,0:T(8,128)(2,1)} %hid_h.1) | copy-start | bytes 294916
  3.7 2.4 %copy-start.2 = (f32[2,1536]{1,0:T(2,128)S(1)}, f32[2,1536]{1,0:T(2,128)}, u32[]{:S(2)}) copy-start(f32[2,1536]{1,0:T(2,128)} %fmod.1) | copy-start | bytes 36868

commit v2 on v1

v2 whole, which is shorter than its diff:
```python
import jax
import jax.numpy as jnp
from jax import lax
from jax.experimental import pallas as pl
from jax.experimental.pallas import tpu as pltpu
from jax.sharding import PartitionSpec as P

HEAD = 64
MICRO = 4
NC = 4
MESH = pl.DeviceIdType.MESH
F32 = jnp.float32
BF16 = jnp.bfloat16


def dot(a, b):
    return jnp.dot(a, b, preferred_element_type=F32)


def dot_nt(a, b):
    return lax.dot_general(a, b, (((1,), (1,)), ((), ())), preferred_element_type=F32)


class Link:
    def __init__(self, send_sem, recv_sem):
        self.send_sem, self.recv_sem, self.used = send_sem, recv_sem, 0

    def take(self):
        index = self.used
        self.used += 1
        return index

    def make(self, index, src, dst, device):
        return pltpu.make_async_remote_copy(
            src_ref=src,
            dst_ref=dst,
            send_sem=self.send_sem.at[index],
            recv_sem=self.recv_sem.at[index],
            device_id=device,
            device_id_type=MESH,
        )


N_LINK = 72
N_LOCAL = 12


def kernel(
    order_h, tlen_h, step_h, hid_h, wq_h, wo_h, st_h, tx_h, mod_h, fmod_h, wf_h, lat_h,
    out_lat, out_kv,
    hx, wraw, wex, wv, kvf, kvs, straw, sex, txraw, tx, wo, nm, at, lhs, nkv, fin, acc, sbuf,
    mod, fmod, wf, lat, order, tlen, step,
    send_sem, recv_sem, loc_sem, go_sem,
):
    sec = lax.axis_index("section")
    seq = lax.axis_index("seq")
    tp = lax.axis_index("tp")
    req = lax.axis_index("req")
    zh = seq // 4
    oh = 1 - zh
    y = seq % 4
    z = zh * 8 + req
    far = req // 4
    hop = 1 - 2 * far
    depth = req + far * (7 - 2 * req)
    xs = [(tp + k) % 4 for k in (1, 2, 3)]
    ys = [(y + k) % 4 for k in (1, 2, 3)]
    xfrom = [(tp + 4 - k) % 4 for k in (1, 2, 3)]
    yfrom = [(y + 4 - k) % 4 for k in (1, 2, 3)]
    xdev = [{"tp": v} for v in xs]
    ydev = [{"seq": zh * 4 + v} for v in ys]
    zdev = {"seq": (seq + 4) % 8}
    core = {"section": 1 - sec}

    def along_z(steps):
        place = (z + steps + 16) % 16
        return {"seq": (place // 8) * 4 + y, "req": place % 8}

    next_dev = along_z(hop)
    prev_dev = along_z(-hop)
    over_dev = along_z(-4 * hop)

    barrier = pltpu.get_barrier_semaphore()
    for device in xdev + ydev + [zdev, core, next_dev, prev_dev, over_dev]:
        pl.semaphore_signal(barrier, inc=1, device_id=device, device_id_type=MESH)

    link = Link(send_sem, recv_sem)
    half_rows = lambda h: pl.ds(h * 128, 128)
    three = range(3)
    i_hx = [link.take() for _ in three]
    i_hz = link.take()
    i_hf = [link.take() for _ in three]
    i_wy = [link.take() for _ in three]
    i_ch = [link.take() for _ in range(NC)]
    i_ex = [link.take() for _ in range(NC)]
    i_wr = [[link.take() for _ in three] for _ in range(NC)]
    i_sy = [link.take() for _ in three]
    i_sz = link.take()
    i_sr = [link.take() for _ in three]
    i_wo = [[link.take() for _ in three] for _ in range(2)]
    i_kv = [link.take() for _ in three]
    i_nk = link.take()
    i_ax = [[link.take() for _ in three] for _ in range(2)]
    i_az = [link.take() for _ in range(2)]
    i_af = [[link.take() for _ in three] for _ in range(2)]
    i_h1 = [[link.take() for _ in range(4)] for _ in range(2)]
    i_fn = link.take()

    def send(index, src, dst, device):
        link.make(index, src, dst, device).start()

    def arrived(index, dst):
        link.make(index, dst, dst, core).wait_recv()

    def sent(index, src):
        link.make(index, src, src, core).wait_send()

    hx_slot = lambda x, h: hx.at[x, half_rows(h), :]

    wo_rows = lambda x, part: wo.at[pl.ds(x * 384 + part * 192, 192), :]
    local = [
        pltpu.make_async_copy(src, dst, loc_sem.at[n])
        for n, (src, dst) in enumerate(
            [
                (wq_h, wraw),
                (hid_h, hx_slot(tp, zh)),
                (st_h, straw),
                (tx_h, txraw),
                (mod_h, mod),
                (order_h, order),
                (tlen_h, tlen),
                (step_h, step),
                (fmod_h, fmod),
                (wf_h, wf),
                (lat_h, lat),
                (wo_h, wo.at[pl.ds(tp * 384, 384), :]),
            ]
        )
    ]
    local[0].start()

    @pl.when(sec == 0)
    def _():
        local[1].start()

    for copy in local[2:]:
        copy.start()

    low = lax.broadcasted_iota(jnp.int32, (1, 128), 1) < HEAD
    single_low = zh == 0
    tiles = [slice(c * 128, c * 128 + 128) for c in range(12)]

    def turn(value):
        return pltpu.roll(value.astype(F32), HEAD, 1)

    def both_singles(k_tile, v_tile):
        turned = turn(v_tile)
        k_tile = k_tile.astype(F32)
        zero = jnp.where(low, k_tile, turned).astype(BF16)
        one = jnp.where(low, turned, k_tile).astype(BF16)
        return jnp.where(single_low, zero, one), jnp.where(single_low, one, zero)

    def both_pairs(first, last):
        return jnp.where(single_low, first, last), jnp.where(single_low, last, first)

    CR = 192 // NC
    w_rows = lambda s: wv.at[pl.ds(s * 192, 192), :]
    w_piece = lambda s, c: wv.at[pl.ds(s * 192 + c * CR, CR), :]
    x_piece = lambda c: wex.at[pl.ds(c * CR, CR), :]

    def put_w(tile, values):
        wv[pl.ds(seq * 192, 192), tiles[tile]] = values[0]
        wex[:, tiles[tile]] = values[1]

    local[0].wait()
    put_w(0, both_pairs(wraw[1, :, tiles[0]], wraw[1, :, tiles[2]]))
    put_w(1, both_singles(wraw[1, :, tiles[1]], wraw[2, :, tiles[1]]))
    put_w(2, both_pairs(wraw[2, :, tiles[0]], wraw[2, :, tiles[2]]))
    put_w(3, both_pairs(wraw[0, :, tiles[0]], wraw[0, :, tiles[2]]))
    put_w(4, [wraw[0, :, tiles[1]]] * 2)

    pl.semaphore_wait(barrier, 11)

    def hidden_send():
        send(i_hz, hid_h, hx_slot(tp, zh), zdev)
        for k in three:
            send(i_hx[k], hid_h, hx_slot(tp, zh), xdev[k])

    def hidden_own():
        local[1].wait()
        for k in three:
            arrived(i_hx[k], hx_slot(xfrom[k], zh))

    def hidden_forward():
        arrived(i_hz, hx_slot(tp, oh))
        for k in three:
            send(i_hf[k], hx_slot(tp, oh), hx_slot(tp, oh), xdev[k])

    def hidden_other():
        for k in three:
            arrived(i_hf[k], hx_slot(xfrom[k], oh))

    def hidden_sent():
        sent(i_hz, hid_h)
        for k in three:
            sent(i_hx[k], hid_h)
            sent(i_hf[k], hx_slot(tp, oh))


    def weights_cross():
        for at_depth, device in ((0, prev_dev), (1, over_dev)):

            @pl.when(depth == at_depth)
            def _(device=device):
                for c in range(NC):
                    pltpu.make_async_remote_copy(
                        src_ref=x_piece(c),
                        dst_ref=w_piece(seq, c),
                        send_sem=send_sem.at[i_ex[c]],
                        recv_sem=recv_sem.at[i_ch[c]],
                        device_id=device,
                        device_id_type=MESH,
                    ).start()

    def weights_y():
        for k in three:
            send(i_wy[k], w_rows(seq), w_rows(seq), ydev[k])

    oseq = oh * 4 + y

    def weights_pass(c):
        arrived(i_ch[c], w_piece(oseq, c))

        @pl.when(depth % 2 == 0)
        def _():
            send(i_ch[c], w_piece(oseq, c), w_piece(oseq, c), next_dev)

    def weights_relay(c):
        for k in three:
            send(i_wr[c][k], w_piece(oseq, c), w_piece(oseq, c), ydev[k])

    def weights_near():
        for k in three:
            arrived(i_wy[k], w_rows(zh * 4 + yfrom[k]))

    def weights_far():
        for c in range(NC):
            for k in three:
                arrived(i_wr[c][k], w_piece(oh * 4 + yfrom[k], c))

    def weights_sent():
        @pl.when(depth < 2)
        def _():
            for c in range(NC):
                sent(i_ex[c], x_piece(c))

        @pl.when(depth % 2 == 0)
        def _():
            for c in range(NC):
                sent(i_ch[c], w_piece(oseq, c))

        for k in three:
            sent(i_wy[k], w_rows(seq))
            for c in range(NC):
                sent(i_wr[c][k], w_piece(oseq, c))

    st_slot = lambda v, h: kvs.at[v, half_rows(h), :]

    def stale_tiles():
        local[2].wait()

        def put(tile, values):
            kvs[y, half_rows(zh), tiles[tile]] = values[0]
            sex[:, tiles[tile]] = values[1]

        put(0, both_pairs(straw[0, :, tiles[0]], straw[0, :, tiles[2]]))
        put(1, both_singles(straw[0, :, tiles[1]], straw[1, :, tiles[1]]))
        put(2, both_pairs(straw[1, :, tiles[0]], straw[1, :, tiles[2]]))

    def text_tiles():
        local[3].wait()
        tx[144:256, :] = jnp.zeros((112, 384), BF16)
        live = slice(0, txraw.shape[1])
        tx[live, tiles[0]] = both_pairs(txraw[0, :, tiles[0]], txraw[0, :, tiles[2]])[0]
        tx[live, tiles[1]] = both_singles(txraw[0, :, tiles[1]], txraw[1, :, tiles[1]])[0]
        tx[live, tiles[2]] = both_pairs(txraw[1, :, tiles[0]], txraw[1, :, tiles[2]])[0]

    def stale_z():
        send(i_sz, sex, st_slot(y, zh), zdev)

    def stale_y():
        for k in three:
            send(i_sy[k], st_slot(y, zh), st_slot(y, zh), ydev[k])

    def stale_relay():
        arrived(i_sz, st_slot(y, oh))
        for k in three:
            send(i_sr[k], st_slot(y, oh), st_slot(y, oh), ydev[k])

    def stale_all():
        for k in three:
            arrived(i_sy[k], st_slot(yfrom[k], zh))
            arrived(i_sr[k], st_slot(yfrom[k], oh))

    def stale_sent():
        sent(i_sz, sex)
        for k in three:
            sent(i_sy[k], st_slot(y, zh))
            sent(i_sr[k], st_slot(y, oh))

    def out_send(part):
        for k in three:
            send(i_wo[part][k], wo_h.at[pl.ds(part * 192, 192), :], wo_rows(tp, part), xdev[k])

    def out_all():
        local[11].wait()
        for k in three:
            for part in range(2):
                arrived(i_wo[part][k], wo_rows(xfrom[k], part))

    def norm_rows(r0, count, shift, scale, store):
        parts = [hx[c, pl.ds(r0, count), :].astype(F32) for c in range(4)]
        total = sum(jnp.sum(part, axis=-1, keepdims=True) for part in parts)
        mean = total * (1.0 / 1536)
        parts = [part - mean for part in parts]
        spread = sum(jnp.sum(part * part, axis=-1, keepdims=True) for part in parts)
        inv = lax.rsqrt(spread * (1.0 / 1536) + 1e-06)
        for c in range(4):
            lanes = slice(c * 384, (c + 1) * 384)
            store(c, (parts[c] * inv * (1.0 + scale(lanes)) + shift(lanes)).astype(BF16))

    def norm_block(h):
        for b in range(4):
            r0 = h * 128 + b * 32

            def store(c, value, r0=r0):
                nm[c // 2, pl.ds(r0, 32), (c % 2) * 384 : (c % 2) * 384 + 384] = value

            norm_rows(r0, 32, lambda l: mod[0, :, l], lambda l: mod[1, :, l], store)

    def go(index):
        pl.semaphore_signal(go_sem.at[index], inc=1, device_id=core, device_id_type=MESH)

    def go_wait(index):
        pl.semaphore_wait(go_sem.at[index], 1)

    @pl.when(sec == 0)
    def _():
        hidden_send()
        weights_cross()
        weights_y()

    @pl.when(sec == 1)
    def _():
        out_send(0)

    stale_tiles()
    for copy in local[4:11]:
        copy.wait()

    @pl.when(sec == 0)
    def _():
        @pl.when(depth == 3)
        def _():
            hidden_forward()

        for c in range(NC):
            weights_pass(c)
            weights_relay(c)

        @pl.when(depth < 3)
        def _():
            hidden_forward()

        stale_z()
        out_send(0)
        out_send(1)
        go(0)
        stale_y()
        hidden_own()
        norm_block(zh)
        text_tiles()
        hidden_other()
        norm_block(oh)

    @pl.when(sec == 1)
    def _():
        text_tiles()
        go_wait(0)
        stale_z()
        weights_cross()
        for c in range(NC):
            weights_pass(c)
        go_wait(1)
        weights_y()
        for c in range(NC):
            weights_relay(c)
        stale_y()
        stale_relay()
        go_wait(2)
        out_send(1)
        for n in range(4):
            arrived(i_h1[0][n], hx.at[n, half_rows(zh), :])
        norm_block(zh)
        for n in range(4):
            arrived(i_h1[1][n], hx.at[n, half_rows(oh), :])
        norm_block(oh)

    segment = lax.broadcasted_iota(jnp.int32, (1, 256), 1) // 32
    rank_of = [
        [sum(jnp.where(order[k, s] == p, k, 0) for k in range(1, MICRO)) for p in range(MICRO)]
        for s in range(8)
    ]
    row_segment = lax.broadcasted_iota(jnp.int32, (256, 1), 0) // 32
    qrank = jnp.zeros((256, 1), jnp.int32)
    kranks = []
    for v in range(4):
        krank = jnp.zeros((1, 256), jnp.int32)
        for j in range(8):
            scalar = rank_of[(j // 4) * 4 + v][j % 4]
            krank = jnp.where(segment == j, scalar, krank)
            qrank = jnp.where((row_segment == j) & (y == v), scalar, qrank)
        kranks.append(krank)
    text_live = lax.broadcasted_iota(jnp.int32, (1, 256), 1) < tlen[0]

    weights_near()
    for c in range(5):
        acc[:, tiles[c]] = dot(nm[zh], wv[pl.ds(zh * 768, 768), tiles[c]])
    weights_far()
    own = kvf.at[y]
    for c in range(5):
        value = acc[:, tiles[c]] + dot(nm[oh], wv[pl.ds(oh * 768, 768), tiles[c]])
        if c < 3:
            kvf[y, :, tiles[c]] = value.astype(BF16)
        else:
            lhs[:, tiles[c - 3]] = value.astype(BF16)
        if c == 2:
            for k in three:
                send(i_kv[k], own, own, ydev[k])
    send(i_nk, kvf.at[y, half_rows(oh), :], nkv, zdev)

    @pl.when(sec == 0)
    def _():
        stale_relay()

    stale_all()
    for k in three:
        arrived(i_kv[k], kvf.at[yfrom[k]])

    @pl.when(sec == 0)
    def _():
        go(1)

    def attend(rb):
        rows = half_rows(rb)
        rank = jnp.where(rb == 0, qrank[0:128], qrank[128:256])
        masks = [kranks[v] <= rank for v in range(4)]
        outs = []
        for j in range(3):
            tile = 0 if j < 2 else 1
            query = lhs[rows, tiles[tile]].astype(F32) * (HEAD ** (-0.5))
            if j == 0:
                keep = low
            elif j == 1:
                keep = jnp.logical_not(low)
            else:
                keep = low == single_low
            query = jnp.where(keep, query, 0.0).astype(BF16)
            kl = tiles[tile]
            vl = tiles[2] if j < 2 else kl
            for v in range(4):
                fresh = dot_nt(query, kvf[v, :, kl])
                stale = dot_nt(query, kvs[v, :, kl])
                sbuf[:, v * 256 : v * 256 + 256] = jnp.where(masks[v], fresh, stale)
            text = dot_nt(query, tx[:, kl])
            sbuf[:, 1024:1280] = jnp.where(text_live, text, -1e30)
            scores = sbuf[...]
            peak = jnp.max(scores, axis=-1, keepdims=True)
            weights = jnp.exp(scores - peak)
            inv = 1.0 / jnp.sum(weights, axis=-1, keepdims=True)
            sbuf[...] = weights * inv
            total = dot(sbuf[:, 1024:1280].astype(BF16), tx[:, vl])
            for v in range(4):
                weights = sbuf[:, v * 256 : v * 256 + 256]
                fresh = jnp.where(masks[v], weights, 0.0).astype(BF16)
                stale = jnp.where(masks[v], 0.0, weights).astype(BF16)
                total = total + dot(fresh, kvf[v, :, vl]) + dot(stale, kvs[v, :, vl])
            outs.append(total)
        at[zh, tp, rb, 0:128, :] = jnp.where(low, outs[0], outs[1]).astype(BF16)
        single = jnp.where(low == single_low, 0.0, outs[2])
        single = single + pltpu.roll(single, HEAD, 1)
        at[zh, tp, rb, 128:192, :] = jnp.where(low, single[0:64], single[64:128]).astype(BF16)

    block = lambda a, x, rb: at.at[a, x, rb]
    attend(oh)
    send(i_az[0], block(zh, tp, oh), block(zh, tp, oh), zdev)

    @pl.when(sec == 0)
    def _():
        for k in three:
            send(i_ax[1][k], block(zh, tp, oh), block(zh, tp, oh), xdev[k])

    attend(zh)

    @pl.when(sec == 0)
    def _():
        send(i_az[1], block(zh, tp, zh), block(zh, tp, zh), zdev)

    for k in three:
        send(i_ax[0][k], block(zh, tp, zh), block(zh, tp, zh), xdev[k])

    arrived(i_nk, nkv)
    mine_kv = [kvf[y, half_rows(zh), tiles[c]] for c in range(3)]
    their_kv = [nkv[:, tiles[c]] for c in range(3)]
    first_kv = [jnp.where(single_low, a, b) for a, b in zip(mine_kv, their_kv)]
    second_kv = [jnp.where(single_low, b, a) for a, b in zip(mine_kv, their_kv)]
    out_kv[0, :, tiles[0]] = first_kv[0]
    out_kv[0, :, tiles[1]] = jnp.where(low, first_kv[1], second_kv[1])
    out_kv[0, :, tiles[2]] = second_kv[0]
    out_kv[1, :, tiles[0]] = first_kv[2]
    out_kv[1, :, tiles[1]] = turn(jnp.where(low, second_kv[1], first_kv[1])).astype(BF16)
    out_kv[1, :, tiles[2]] = second_kv[2]

    arrived(i_az[0], block(oh, tp, zh))
    for k in three:
        send(i_af[0][k], block(oh, tp, zh), block(oh, tp, zh), xdev[k])

    @pl.when(sec == 0)
    def _():
        arrived(i_az[1], block(oh, tp, oh))
        for k in three:
            send(i_af[1][k], block(oh, tp, oh), block(oh, tp, oh), xdev[k])
        hidden_sent()

    def out_rows(part, rb):
        for k in three:
            arrived(i_ax[part][k], block(zh, xfrom[k], rb))
        for k in three:
            arrived(i_af[part][k], block(oh, xfrom[k], rb))
        for x in range(4):
            lhs[0:128, tiles[3 * x]] = at[0, x, rb, 0:128, :]
            lhs[0:128, tiles[3 * x + 2]] = at[1, x, rb, 0:128, :]
            a = at[0, x, rb, 128:192, :]
            b = at[1, x, rb, 128:192, :]
            lhs[0:64, tiles[3 * x + 1]] = jnp.where(low, a.astype(F32), turn(b)).astype(BF16)
            lhs[64:128, tiles[3 * x + 1]] = jnp.where(low, turn(a), b.astype(F32)).astype(BF16)
        for n in range(4):
            lanes = slice(n * 384, n * 384 + 384)
            branch = dot(lhs[0:128, :], wo[:, lanes])
            rows = half_rows(rb)
            hx[n, rows, :] = (hx[n, rows, :].astype(F32) + mod[2, :, lanes] * branch).astype(BF16)

            @pl.when(sec == 0)
            def _():
                send(i_h1[part][n], hx.at[n, rows, :], hx.at[n, rows, :], core)

    out_all()
    out_rows(0, zh)

    @pl.when(sec == 0)
    def _():
        out_rows(1, oh)
        go(2)

    @pl.when(sec == 1)
    def _():
        for b in range(4):

            def store(c, value, b=b):
                fin[b * 32 : b * 32 + 32, c * 384 : c * 384 + 384] = value

            norm_rows(
                zh * 128 + b * 32, 32, lambda l: fmod[0:1, l], lambda l: fmod[1:2, l], store
            )
        send(i_fn, fin, fin, core)

    @pl.when(sec == 0)
    def _():
        arrived(i_fn, fin)

    out_lat[...] = lat[...] + step[0] * dot_nt(wf[...], fin[...])

    @pl.when(sec == 0)
    def _():
        for part, rb in ((0, zh), (1, oh)):
            for n in range(4):
                sent(i_h1[part][n], hx.at[n, half_rows(rb), :])
        sent(i_az[1], block(zh, tp, zh))
        for k in three:
            sent(i_ax[1][k], block(zh, tp, oh))
            sent(i_af[1][k], block(oh, tp, oh))

    @pl.when(sec == 1)
    def _():
        sent(i_fn, fin)

    weights_sent()
    stale_sent()
    for k in three:
        for part in range(2):
            sent(i_wo[part][k], wo_rows(tp, part))
        sent(i_kv[k], own)
        sent(i_ax[0][k], block(zh, tp, zh))
        sent(i_af[0][k], block(oh, tp, zh))
    sent(i_nk, nkv)
    sent(i_az[0], block(zh, tp, oh))


def body(
    hidden, latent, w_qkv, w_out, modulation, final_mod, w_final, stale_kv, text_kv, text_len,
    patch_order, step_size,
):
    vmem = pl.BlockSpec(memory_space=pltpu.VMEM)
    any_ = pl.BlockSpec(memory_space=pltpu.HBM)
    text = text_kv[0]
    lat_next, kv_next = pl.pallas_call(
        kernel,
        out_shape=(
            jax.ShapeDtypeStruct((8, 128), F32),
            jax.ShapeDtypeStruct((2, 128, 384), BF16),
        ),
        in_specs=[any_] * 12,
        out_specs=(vmem, vmem),
        scratch_shapes=[
            pltpu.VMEM((4, 256, 384), BF16),
            pltpu.VMEM((3, 192, 384), BF16),
            pltpu.VMEM((192, 640), BF16),
            pltpu.VMEM((1536, 640), BF16),
            pltpu.VMEM((4, 256, 384), BF16),
            pltpu.VMEM((4, 256, 384), BF16),
            pltpu.VMEM((2, 128, 384), BF16),
            pltpu.VMEM((128, 384), BF16),
            pltpu.VMEM(text.shape, BF16),
            pltpu.VMEM((256, 384), BF16),
            pltpu.VMEM((1536, 1536), BF16),
            pltpu.VMEM((2, 256, 768), BF16),
            pltpu.VMEM((2, 4, 2, 192, 128), BF16),
            pltpu.VMEM((256, 1536), BF16),
            pltpu.VMEM((128, 384), BF16),
            pltpu.VMEM((128, 1536), BF16),
            pltpu.VMEM((256, 640), F32),
            pltpu.VMEM((128, 1280), F32),
            pltpu.VMEM((3, 1, 1536), F32),
            pltpu.VMEM((2, 1536), F32),
            pltpu.VMEM((8, 1536), BF16),
            pltpu.VMEM((8, 128), F32),
            pltpu.SMEM((4, 8), jnp.int32),
            pltpu.SMEM((1,), jnp.int32),
            pltpu.SMEM((1,), F32),
            pltpu.SemaphoreType.DMA((N_LINK,)),
            pltpu.SemaphoreType.DMA((N_LINK,)),
            pltpu.SemaphoreType.DMA((N_LOCAL,)),
            pltpu.SemaphoreType.REGULAR((3,)),
        ],
        compiler_params=pltpu.CompilerParams(
            collective_id=0, has_side_effects=True, vmem_limit_bytes=63 << 20
        ),
        name="both_layers",
    )(
        patch_order.T, text_len, step_size, hidden, w_qkv[0].transpose(1, 0, 2), w_out[0],
        stale_kv[0], text, modulation.transpose(1, 0, 2), final_mod, w_final.T, latent.T,
    )
    return lat_next.T, kv_next[None]


def solution(mesh):
    return jax.shard_map(
        body,
        mesh=mesh,
        in_specs=(
            P(("req", "seq"), "tp"),
            P(("req", "seq"), ("section", "tp")),
            P("section", "seq", None, "tp"),
            P("section", "tp", None),
            P("section", None, None),
            P(),
            P(None, ("section", "tp")),
            P("section", None, ("req", "seq"), "tp"),
            P("section", None, "req", "tp"),
            P("req"),
            P("req", None),
            P(),
        ),
        out_specs=(P(("req", "seq"), ("section", "tp")), P("section", None, ("req", "seq"), "tp")),
        check_vma=False,
    )
```

time: 132 us -> 109 us (0.83)
  the two profiles are of different devices: /device:TPU:113 before, /device:TPU:1 now
where the time goes in v2:
time: 109 us
  Pallas kernels  103 us (94%)
  local copies, waits for them, and re-layouts  4.55 us (4%)
  between operations  1.93 us (2%)
    pallas_call x1, Pallas kernels, body(): pl.pallas_call(kernel, out_shape=(jax.ShapeDtypeStruct((8, 128), F32), ja...  103 us
    unnamed x3, local copies, waits for them, and re-layouts  4.55 us

profile of v2, /device:TPU:1, one launch (start us, length us, event | category | flops | bytes accessed | tf_op | source)
XLA Modules:
  0.0 109.1 jit_solution(12134504706477399967)
XLA Ops:
  1.9 1.7 %copy.16 = bf16[1,2,154,384]{3,2,1,0:T(8,128)(2,1)} copy(bf16[1,2,154,384]{3,1,2,0:T(2,128)(2,1)} %param.20) | data formatting | bytes 473088 | tf_op args[8]
  3.6 102.6 %both_layers.1 = (f32[8,128]{1,0:T(8,128)}, bf16[2,128,384]{2,1,0:T(8,128)(2,1)}) custom-call(s32[4,8]{1,0:T(4,128)} %bitcast.23, s32[1]{0:T(128)S(6)} %copy.19.tlen_h, f32[1]{0:T(128)S(6)} %copy.20.step_h, bf16[128,384]{1,0:T(8,128)(2,1)} %hid_h.1, bf16[3,192,384]{2,1,0:T(8,128)(2,1)} %bitcast.16, bf16[384,1536]{1,0:T(8,128)(2,1)} %bitcast.14, ...), custom_call_target="tpu_custom_call" | custom-call | tf_op jit(solution)/shard_map/both_layers/pallas_call | solution.py:616
  106.2 1.3 %copy.21 = f32[128,8]{0,1:T(8,128)} copy(f32[128,8]{0,1:T(8,128)} %bitcast.22) | data formatting | bytes 8192
  107.5 1.6 %copy.22 = bf16[1,2,128,384]{3,2,1,0:T(8,128)(2,1)} copy(bf16[1,2,128,384]{3,2,1,0:T(8,128)(2,1)} %bitcast.17) | data formatting | bytes 393216

commit v3 on v2

--- a/solution.py
+++ b/solution.py
@@ -7,7 +7,8 @@
 
 HEAD = 64
 MICRO = 4
-NC = 4
+NC = 5
+HC = 2
 MESH = pl.DeviceIdType.MESH
 F32 = jnp.float32
 BF16 = jnp.bfloat16
@@ -41,15 +42,15 @@
         )
 
 
-N_LINK = 72
+N_LINK = 112
 N_LOCAL = 12
 
 
 def kernel(
     order_h, tlen_h, step_h, hid_h, wq_h, wo_h, st_h, tx_h, mod_h, fmod_h, wf_h, lat_h,
     out_lat, out_kv,
-    hx, wraw, wex, wv, kvf, kvs, straw, sex, txraw, tx, wo, nm, at, lhs, nkv, fin, acc, sbuf,
-    mod, fmod, wf, lat, order, tlen, step,
+    hx, hland, wraw, wex, wv, kvf, kvs, straw, sex, txraw, tx, wo, nm, at, lhs, nkv, fin, acc, sbuf,
+    mod, fmod, wf, vel, lat, order, tlen, step,
     send_sem, recv_sem, loc_sem, go_sem,
 ):
     sec = lax.axis_index("section")
@@ -71,40 +72,42 @@
     ydev = [{"seq": zh * 4 + v} for v in ys]
     zdev = {"seq": (seq + 4) % 8}
     core = {"section": 1 - sec}
+    xcross = [{"tp": v, "section": 1 - sec} for v in xs]
 
     def along_z(steps):
         place = (z + steps + 16) % 16
         return {"seq": (place // 8) * 4 + y, "req": place % 8}
 
-    next_dev = along_z(hop)
-    prev_dev = along_z(-hop)
-    over_dev = along_z(-4 * hop)
+    cross_dev = along_z(-2 * hop)
+    pass_dev = [along_z(hop), along_z(2 * hop), along_z(-hop)]
 
     barrier = pltpu.get_barrier_semaphore()
-    for device in xdev + ydev + [zdev, core, next_dev, prev_dev, over_dev]:
+    for device in xdev + xcross + ydev + [zdev, core, cross_dev] + pass_dev:
         pl.semaphore_signal(barrier, inc=1, device_id=device, device_id_type=MESH)
 
     link = Link(send_sem, recv_sem)
     half_rows = lambda h: pl.ds(h * 128, 128)
     three = range(3)
     i_hx = [link.take() for _ in three]
-    i_hz = link.take()
-    i_hf = [link.take() for _ in three]
+    i_hz = [link.take() for _ in range(HC)]
+    i_hf = [[link.take() for _ in range(4)] for _ in range(HC)]
     i_wy = [link.take() for _ in three]
     i_ch = [link.take() for _ in range(NC)]
     i_ex = [link.take() for _ in range(NC)]
+    i_ps = [[link.take() for _ in three] for _ in range(NC)]
     i_wr = [[link.take() for _ in three] for _ in range(NC)]
     i_sy = [link.take() for _ in three]
     i_sz = link.take()
     i_sr = [link.take() for _ in three]
     i_wo = [[link.take() for _ in three] for _ in range(2)]
-    i_kv = [link.take() for _ in three]
+    i_kv = [[link.take() for _ in three] for _ in range(3)]
     i_nk = link.take()
     i_ax = [[link.take() for _ in three] for _ in range(2)]
     i_az = [link.take() for _ in range(2)]
     i_af = [[link.take() for _ in three] for _ in range(2)]
     i_h1 = [[link.take() for _ in range(4)] for _ in range(2)]
     i_fn = link.take()
+    i_wf = link.take()
 
     def send(index, src, dst, device):
         link.make(index, src, dst, device).start()
@@ -117,7 +120,8 @@
 
     hx_slot = lambda x, h: hx.at[x, half_rows(h), :]
 
-    wo_rows = lambda x, part: wo.at[pl.ds(x * 384 + part * 192, 192), :]
+    wo_part = lambda start, part: pl.ds(start + part * 96, (96, 288)[part])
+    wo_rows = lambda x, part: wo.at[wo_part(x * 384, part), :]
     local = [
         pltpu.make_async_copy(src, dst, loc_sem.at[n])
         for n, (src, dst) in enumerate(
@@ -131,7 +135,7 @@
                 (tlen_h, tlen),
                 (step_h, step),
                 (fmod_h, fmod),
-                (wf_h, wf),
+                (wf_h, wf.at[0]),
                 (lat_h, lat),
                 (wo_h, wo.at[pl.ds(tp * 384, 384), :]),
             ]
@@ -163,14 +167,13 @@
     def both_pairs(first, last):
         return jnp.where(single_low, first, last), jnp.where(single_low, last, first)
 
-    CR = 192 // NC
-    w_rows = lambda s: wv.at[pl.ds(s * 192, 192), :]
-    w_piece = lambda s, c: wv.at[pl.ds(s * 192 + c * CR, CR), :]
-    x_piece = lambda c: wex.at[pl.ds(c * CR, CR), :]
+    w_rows = lambda s: wv.at[:, pl.ds(s * 192, 192), :]
+    w_piece = lambda s, c: wv.at[c, pl.ds(s * 192, 192), :]
+    x_piece = lambda c: wex.at[c]
 
     def put_w(tile, values):
-        wv[pl.ds(seq * 192, 192), tiles[tile]] = values[0]
-        wex[:, tiles[tile]] = values[1]
+        wv[tile, pl.ds(seq * 192, 192), :] = values[0]
+        wex[tile] = values[1]
 
     local[0].wait()
     put_w(0, both_pairs(wraw[1, :, tiles[0]], wraw[1, :, tiles[2]]))
@@ -179,10 +182,13 @@
     put_w(3, both_pairs(wraw[0, :, tiles[0]], wraw[0, :, tiles[2]]))
     put_w(4, [wraw[0, :, tiles[1]]] * 2)
 
-    pl.semaphore_wait(barrier, 11)
+    pl.semaphore_wait(barrier, 15)
+
+    HR = 128 // HC
+    h_piece = lambda c: pl.ds(c * HR, HR)
+    h_slot = lambda x, h, c: hx.at[x, pl.ds(h * 128 + c * HR, HR), :]
 
     def hidden_send():
-        send(i_hz, hid_h, hx_slot(tp, zh), zdev)
         for k in three:
             send(i_hx[k], hid_h, hx_slot(tp, zh), xdev[k])
 
@@ -191,36 +197,42 @@
         for k in three:
             arrived(i_hx[k], hx_slot(xfrom[k], zh))
 
+    def hidden_cross():
+        for c in range(HC):
+            send(i_hz[c], hid_h.at[h_piece(c), :], hland.at[h_piece(c), :], zdev)
+
     def hidden_forward():
-        arrived(i_hz, hx_slot(tp, oh))
-        for k in three:
-            send(i_hf[k], hx_slot(tp, oh), hx_slot(tp, oh), xdev[k])
+        for c in range(HC):
+            arrived(i_hz[c], hland.at[h_piece(c), :])
+            for k, device in enumerate(xcross + [core]):
+                send(i_hf[c][k], hland.at[h_piece(c), :], h_slot(tp, oh, c), device)
 
     def hidden_other():
-        for k in three:
-            arrived(i_hf[k], hx_slot(xfrom[k], oh))
+        for c in range(HC):
+            for k in range(4):
+                arrived(i_hf[c][k], h_slot((xfrom + [tp])[k], oh, c))
 
     def hidden_sent():
-        sent(i_hz, hid_h)
-        for k in three:
-            sent(i_hx[k], hid_h)
-            sent(i_hf[k], hx_slot(tp, oh))
-
+        for c in range(HC):
+            sent(i_hz[c], hid_h.at[h_piece(c), :])
+            for k in range(4):
+                sent(i_hf[c][k], hland.at[h_piece(c), :])
+
+    def weights_send(index, src, dst, device, c):
+        return pltpu.make_async_remote_copy(
+            src_ref=src,
+            dst_ref=dst,
+            send_sem=send_sem.at[index],
+            recv_sem=recv_sem.at[i_ch[c]],
+            device_id=device,
+            device_id_type=MESH,
+        )
 
     def weights_cross():
-        for at_depth, device in ((0, prev_dev), (1, over_dev)):
-
-            @pl.when(depth == at_depth)
-            def _(device=device):
-                for c in range(NC):
-                    pltpu.make_async_remote_copy(
-                        src_ref=x_piece(c),
-                        dst_ref=w_piece(seq, c),
-                        send_sem=send_sem.at[i_ex[c]],
-                        recv_sem=recv_sem.at[i_ch[c]],
-                        device_id=device,
-                        device_id_type=MESH,
-                    ).start()
+        @pl.when(depth == 0)
+        def _():
+            for c in range(NC):
+                weights_send(i_ex[c], x_piece(c), w_piece(seq, c), cross_dev, c).start()
 
     def weights_y():
         for k in three:
@@ -231,9 +243,11 @@
     def weights_pass(c):
         arrived(i_ch[c], w_piece(oseq, c))
 
-        @pl.when(depth % 2 == 0)
+        @pl.when(depth == 1)
         def _():
-            send(i_ch[c], w_piece(oseq, c), w_piece(oseq, c), next_dev)
+            piece = w_piece(oseq, c)
+            for k in three:
+                weights_send(i_ps[c][k], piece, piece, pass_dev[k], c).start()
 
     def weights_relay(c):
         for k in three:
@@ -243,21 +257,21 @@
         for k in three:
             arrived(i_wy[k], w_rows(zh * 4 + yfrom[k]))
 
-    def weights_far():
-        for c in range(NC):
-            for k in three:
-                arrived(i_wr[c][k], w_piece(oh * 4 + yfrom[k], c))
+    def weights_far(c):
+        for k in three:
+            arrived(i_wr[c][k], w_piece(oh * 4 + yfrom[k], c))
 
     def weights_sent():
-        @pl.when(depth < 2)
+        @pl.when(depth == 0)
         def _():
             for c in range(NC):
                 sent(i_ex[c], x_piece(c))
 
-        @pl.when(depth % 2 == 0)
+        @pl.when(depth == 1)
         def _():
             for c in range(NC):
-                sent(i_ch[c], w_piece(oseq, c))
+                for k in three:
+                    sent(i_ps[c][k], w_piece(oseq, c))
 
         for k in three:
             sent(i_wy[k], w_rows(seq))
@@ -280,10 +294,10 @@
     def text_tiles():
         local[3].wait()
         tx[144:256, :] = jnp.zeros((112, 384), BF16)
-        live = slice(0, txraw.shape[1])
-        tx[live, tiles[0]] = both_pairs(txraw[0, :, tiles[0]], txraw[0, :, tiles[2]])[0]
-        tx[live, tiles[1]] = both_singles(txraw[0, :, tiles[1]], txraw[1, :, tiles[1]])[0]
-        tx[live, tiles[2]] = both_pairs(txraw[1, :, tiles[0]], txraw[1, :, tiles[2]])[0]
+        live = slice(0, txraw.shape[0])
+        tx[live, tiles[0]] = both_pairs(txraw[:, 0, tiles[0]], txraw[:, 0, tiles[2]])[0]
+        tx[live, tiles[1]] = both_singles(txraw[:, 0, tiles[1]], txraw[:, 1, tiles[1]])[0]
+        tx[live, tiles[2]] = both_pairs(txraw[:, 1, tiles[0]], txraw[:, 1, tiles[2]])[0]
 
     def stale_z():
         send(i_sz, sex, st_slot(y, zh), zdev)
@@ -310,7 +324,7 @@
 
     def out_send(part):
         for k in three:
-            send(i_wo[part][k], wo_h.at[pl.ds(part * 192, 192), :], wo_rows(tp, part), xdev[k])
+            send(i_wo[part][k], wo_h.at[wo_part(0, part), :], wo_rows(tp, part), xdev[k])
 
     def out_all():
         local[11].wait()
@@ -346,12 +360,13 @@
 
     @pl.when(sec == 0)
     def _():
+        weights_cross()
         hidden_send()
-        weights_cross()
         weights_y()
 
     @pl.when(sec == 1)
     def _():
+        hidden_cross()
         out_send(0)
 
     stale_tiles()
@@ -360,22 +375,13 @@
 
     @pl.when(sec == 0)
     def _():
-        @pl.when(depth == 3)
-        def _():
-            hidden_forward()
-
+        send(i_wf, wf.at[0], wf.at[1], core)
         for c in range(NC):
             weights_pass(c)
             weights_relay(c)
-
-        @pl.when(depth < 3)
-        def _():
-            hidden_forward()
-
         stale_z()
         out_send(0)
         out_send(1)
-        go(0)
         stale_y()
         hidden_own()
         norm_block(zh)
@@ -386,6 +392,7 @@
     @pl.when(sec == 1)
     def _():
         text_tiles()
+        hidden_forward()
         go_wait(0)
         stale_z()
         weights_cross()
@@ -425,27 +432,29 @@
 
     weights_near()
     for c in range(5):
-        acc[:, tiles[c]] = dot(nm[zh], wv[pl.ds(zh * 768, 768), tiles[c]])
-    weights_far()
-    own = kvf.at[y]
+        acc[:, tiles[c]] = dot(nm[zh], wv[c, pl.ds(zh * 768, 768), :])
+    kv_tile = lambda v, c: kvf.at[v, :, tiles[c]]
     for c in range(5):
-        value = acc[:, tiles[c]] + dot(nm[oh], wv[pl.ds(oh * 768, 768), tiles[c]])
+        weights_far(c)
+        value = acc[:, tiles[c]] + dot(nm[oh], wv[c, pl.ds(oh * 768, 768), :])
         if c < 3:
             kvf[y, :, tiles[c]] = value.astype(BF16)
         else:
             lhs[:, tiles[c - 3]] = value.astype(BF16)
-        if c == 2:
+        if c < 3:
             for k in three:
-                send(i_kv[k], own, own, ydev[k])
+                send(i_kv[c][k], kv_tile(y, c), kv_tile(y, c), ydev[k])
     send(i_nk, kvf.at[y, half_rows(oh), :], nkv, zdev)
 
     @pl.when(sec == 0)
     def _():
+        go(0)
         stale_relay()
 
     stale_all()
-    for k in three:
-        arrived(i_kv[k], kvf.at[yfrom[k]])
+    for c in range(3):
+        for k in three:
+            arrived(i_kv[c][k], kv_tile(yfrom[k], c))
 
     @pl.when(sec == 0)
     def _():
@@ -530,7 +539,8 @@
         arrived(i_az[1], block(oh, tp, oh))
         for k in three:
             send(i_af[1][k], block(oh, tp, oh), block(oh, tp, oh), xdev[k])
-        hidden_sent()
+        for k in three:
+            sent(i_hx[k], hid_h)
 
     def out_rows(part, rb):
         for k in three:
@@ -572,19 +582,23 @@
             norm_rows(
                 zh * 128 + b * 32, 32, lambda l: fmod[0:1, l], lambda l: fmod[1:2, l], store
             )
-        send(i_fn, fin, fin, core)
-
-    @pl.when(sec == 0)
-    def _():
-        arrived(i_fn, fin)
-
-    out_lat[...] = lat[...] + step[0] * dot_nt(wf[...], fin[...])
+        arrived(i_wf, wf.at[1])
+        theirs = dot_nt(wf[1], fin[...])
+        vel[0] = theirs
+        send(i_fn, vel.at[0], vel.at[1], core)
+        out_lat[...] = lat[...] + step[0] * dot_nt(wf[0], fin[...])
+
+    @pl.when(sec == 0)
+    def _():
+        arrived(i_fn, vel.at[1])
+        out_lat[...] = lat[...] + step[0] * vel[1]
 
     @pl.when(sec == 0)
     def _():
         for part, rb in ((0, zh), (1, oh)):
             for n in range(4):
                 sent(i_h1[part][n], hx.at[n, half_rows(rb), :])
+        sent(i_wf, wf.at[0])
         sent(i_az[1], block(zh, tp, zh))
         for k in three:
             sent(i_ax[1][k], block(zh, tp, oh))
@@ -592,14 +606,16 @@
 
     @pl.when(sec == 1)
     def _():
-        sent(i_fn, fin)
+        sent(i_fn, vel.at[0])
+        hidden_sent()
 
     weights_sent()
     stale_sent()
     for k in three:
         for part in range(2):
             sent(i_wo[part][k], wo_rows(tp, part))
-        sent(i_kv[k], own)
+        for c in range(3):
+            sent(i_kv[c][k], kv_tile(y, c))
         sent(i_ax[0][k], block(zh, tp, zh))
         sent(i_af[0][k], block(oh, tp, zh))
     sent(i_nk, nkv)
@@ -612,7 +628,7 @@
 ):
     vmem = pl.BlockSpec(memory_space=pltpu.VMEM)
     any_ = pl.BlockSpec(memory_space=pltpu.HBM)
-    text = text_kv[0]
+    text = text_kv[0].transpose(1, 0, 2)
     lat_next, kv_next = pl.pallas_call(
         kernel,
         out_shape=(
@@ -623,9 +639,10 @@
         out_specs=(vmem, vmem),
         scratch_shapes=[
             pltpu.VMEM((4, 256, 384), BF16),
+            pltpu.VMEM((128, 384), BF16),
             pltpu.VMEM((3, 192, 384), BF16),
-            pltpu.VMEM((192, 640), BF16),
-            pltpu.VMEM((1536, 640), BF16),
+            pltpu.VMEM((5, 192, 128), BF16),
+            pltpu.VMEM((5, 1536, 128), BF16),
             pltpu.VMEM((4, 256, 384), BF16),
             pltpu.VMEM((4, 256, 384), BF16),
             pltpu.VMEM((2, 128, 384), BF16),
@@ -642,7 +659,8 @@
             pltpu.VMEM((128, 1280), F32),
             pltpu.VMEM((3, 1, 1536), F32),
             pltpu.VMEM((2, 1536), F32),
-            pltpu.VMEM((8, 1536), BF16),
+            pltpu.VMEM((2, 8, 1536), BF16),
+            pltpu.VMEM((2, 8, 128), F32),
             pltpu.VMEM((8, 128), F32),
             pltpu.SMEM((4, 8), jnp.int32),
             pltpu.SMEM((1,), jnp.int32),

time: 109 us -> 101 us (0.927)
  Pallas kernels: 103 us -> 96.1 us
  local copies, waits for them, and re-layouts: 4.55 us -> 2.89 us
    pallas_call x1, Pallas kernels: 103 us -> 96.1 us  [body(): pl.pallas_call(kernel, out_shape=(jax.ShapeDtypeStruct((8, 128), F32), ja...]
    unnamed x3 -> x2, local copies, waits for them, and re-layouts: 4.55 us -> 2.89 us
where the time goes in v3:
time: 101 us
  Pallas kernels  96.1 us (95%)
  local copies, waits for them, and re-layouts  2.89 us (3%)
  between operations  1.93 us (2%)
    pallas_call x1, Pallas kernels, body(): pl.pallas_call(kernel, out_shape=(jax.ShapeDtypeStruct((8, 128), F32), ja...  96.1 us
    unnamed x2, local copies, waits for them, and re-layouts  2.89 us

profile of v3, /device:TPU:1, one launch (start us, length us, event | category | flops | bytes accessed | tf_op | source)
XLA Modules:
  0.0 101.0 jit_solution(15899838462851914073)
XLA Ops:
  1.9 96.1 %both_layers.1 = (f32[8,128]{1,0:T(8,128)}, bf16[2,128,384]{2,1,0:T(8,128)(2,1)}) custom-call(s32[4,8]{1,0:T(4,128)} %bitcast.23, s32[1]{0:T(128)S(6)} %copy.16.tlen_h, f32[1]{0:T(128)S(6)} %copy.17.step_h, bf16[128,384]{1,0:T(8,128)(2,1)} %hid_h.1, bf16[3,192,384]{2,1,0:T(8,128)(2,1)} %bitcast.15, bf16[384,1536]{1,0:T(8,128)(2,1)} %bitcast.14, ...), custom_call_target="tpu_custom_call" | custom-call | tf_op jit(solution)/shard_map/both_layers/pallas_call | solution.py:632
  98.1 1.3 %copy.18 = f32[128,8]{0,1:T(8,128)} copy(f32[128,8]{0,1:T(8,128)} %bitcast.22) | data formatting | bytes 8192
  99.3 1.6 %copy.19 = bf16[1,2,128,384]{3,2,1,0:T(8,128)(2,1)} copy(bf16[1,2,128,384]{3,2,1,0:T(8,128)(2,1)} %bitcast.18) | data formatting | bytes 393216

commit v4 on v3

--- a/solution.py
+++ b/solution.py
@@ -396,13 +396,23 @@
         go_wait(0)
         stale_z()
         weights_cross()
-        for c in range(NC):
-            weights_pass(c)
+
+        @pl.when(depth == 1)
+        def _():
+            for c in range(NC):
+                weights_pass(c)
+
         go_wait(1)
         weights_y()
+        stale_y()
+
+        @pl.when(depth != 1)
+        def _():
+            for c in range(NC):
+                arrived(i_ch[c], w_piece(oseq, c))
+
         for c in range(NC):
             weights_relay(c)
-        stale_y()
         stale_relay()
         go_wait(2)
         out_send(1)
@@ -671,12 +681,17 @@
             pltpu.SemaphoreType.REGULAR((3,)),
         ],
         compiler_params=pltpu.CompilerParams(
-            collective_id=0, has_side_effects=True, vmem_limit_bytes=63 << 20
+            collective_id=0, has_side_effects=True, vmem_limit_bytes=48 << 20
         ),
         name="both_layers",
     )(
-        patch_order.T, text_len, step_size, hidden, w_qkv[0].transpose(1, 0, 2), w_out[0],
-        stale_kv[0], text, modulation.transpose(1, 0, 2), final_mod, w_final.T, latent.T,
+        *[
+            pltpu.with_memory_space_constraint(value, pltpu.HBM) if value.ndim > 1 else value
+            for value in (
+                patch_order.T, text_len, step_size, hidden, w_qkv[0].transpose(1, 0, 2), w_out[0],
+                stale_kv[0], text, modulation.transpose(1, 0, 2), final_mod, w_final.T, latent.T,
+            )
+        ]
     )
     return lat_next.T, kv_next[None]
 

time: 101 us -> 96.6 us (0.956)
  Pallas kernels: 96.1 us -> 92.7 us
  local copies, waits for them, and re-layouts: 2.89 us -> 1.27 us
    pallas_call x1, Pallas kernels: 96.1 us -> 92.7 us  [body(): pl.pallas_call(kernel, out_shape=(jax.ShapeDtypeStruct((8, 128), F32), ja...]
    unnamed x2, local copies, waits for them, and re-layouts: 2.89 us -> 1.27 us
where the time goes in v4:
time: 96.6 us; the launch traced here: 96 us
  Pallas kernels  92.7 us (96%)
  between operations  1.93 us (2%)
  local copies, waits for them, and re-layouts  1.27 us (1%)
    pallas_call x1, Pallas kernels, body(): pl.pallas_call(kernel, out_shape=(jax.ShapeDtypeStruct((8, 128), F32), ja...  92.7 us

profile of v4, /device:TPU:1, one launch (start us, length us, event | category | flops | bytes accessed | tf_op | source)
XLA Modules:
  0.0 96.0 jit_solution(14202797664135513979)
XLA Ops:
  1.9 92.7 %both_layers.1 = (f32[8,128]{1,0:T(8,128)S(1)}, bf16[2,128,384]{2,1,0:T(8,128)(2,1)S(1)}) custom-call(s32[4,8]{1,0:T(4,128)} %bitcast.23, s32[1]{0:T(128)S(6)} %copy.16.tlen_h, f32[1]{0:T(128)S(6)} %copy.17.step_h, bf16[128,384]{1,0:T(8,128)(2,1)} %hid_h.1, bf16[3,192,384]{2,1,0:T(8,128)(2,1)} %bitcast.17, bf16[384,1536]{1,0:T(8,128)(2,1)} %bitcast.16, ...), custom_call_target="tpu_custom_call" | custom-call | tf_op jit(solution)/shard_map/both_layers/pallas_call | solution.py:642
  94.7 0.6 copy.18
  95.3 0.7 copy.19

commit v5 on v4

--- a/solution.py
+++ b/solution.py
@@ -79,7 +79,7 @@
         return {"seq": (place // 8) * 4 + y, "req": place % 8}
 
     cross_dev = along_z(-2 * hop)
-    pass_dev = [along_z(hop), along_z(2 * hop), along_z(-hop)]
+    pass_dev = [along_z(-hop), along_z(2 * hop), along_z(hop)]
 
     barrier = pltpu.get_barrier_semaphore()
     for device in xdev + xcross + ydev + [zdev, core, cross_dev] + pass_dev:

time: 96.6 us -> 96.7 us (level)
  no operation moved by 1% of the time
where the time goes in v5:
time: 96.7 us; the launch traced here: 95.7 us
  Pallas kernels  92.5 us (96%)
  between operations  1.93 us (2%)
  local copies, waits for them, and re-layouts  1.27 us (1%)
    pallas_call x1, Pallas kernels, body(): pl.pallas_call(kernel, out_shape=(jax.ShapeDtypeStruct((8, 128), F32), ja...  92.5 us

profile of v5, /device:TPU:1, one launch (start us, length us, event | category | flops | bytes accessed | tf_op | source)
XLA Modules:
  0.0 95.7 jit_solution(7962112287433562626)
XLA Ops:
  1.9 92.5 %both_layers.1 = (f32[8,128]{1,0:T(8,128)S(1)}, bf16[2,128,384]{2,1,0:T(8,128)(2,1)S(1)}) custom-call(s32[4,8]{1,0:T(4,128)} %bitcast.23, s32[1]{0:T(128)S(6)} %copy.16.tlen_h, f32[1]{0:T(128)S(6)} %copy.17.step_h, bf16[128,384]{1,0:T(8,128)(2,1)} %hid_h.1, bf16[3,192,384]{2,1,0:T(8,128)(2,1)} %bitcast.17, bf16[384,1536]{1,0:T(8,128)(2,1)} %bitcast.16, ...), custom_call_target="tpu_custom_call" | custom-call | tf_op jit(solution)/shard_map/both_layers/pallas_call | solution.py:642
  94.5 0.6 copy.18
  95.1 0.7 copy.19
